TPU v7x, 32 devices: a whole 2x2x4 slice. The times are simulated.
32 devices in a mesh: tok: 8 (over z, y), vocab: 4 (over x, core).
Axes of the slice: x: 2, y: 2, z: 4, core: 2. Of those that a mesh axis runs over, the one named last changes fastest.
Arguments:
- hidden: bfloat16 [12288, 2048], P('tok')
- gain: float32 [2048], replicated, may hold values from 0.1 to 1.9
- head: bfloat16 [16384, 2048], P(('tok', 'vocab'))
- targets: int32 [12288], P('tok'), may hold values from 0 to 16383
- lengths: int32 [64], P('tok'), may hold values from 1 to 383, as said below
- group_map: int32 [64, 1], P('tok'), may hold values from 0 to 7
Outputs:
- logprob: float32 [12288], P(('tok', 'vocab'))
- entropy: float32 [12288], P(('tok', 'vocab'))
- centered: float32 [64], P(('tok', 'vocab'))
Inputs may be any that keep to these rules, and one draw needn't show every extreme that they name: `lengths`: the 8 requests of one index of tok hold 960 + e tokens in all and those of the index half the axis away hold 960 - e, for some e from 0 to 576; some index holds exactly 1536. `group_map`: every group number names one or more requests.
All inputs are finite; a program needn't handle non-finite values.
Results may differ from a plain program's by a relative error of at most 0.0003.
The roundings to bfloat16 on the way count: a program that leaves them out, or rounds other values in their place, can miss the bound.
Values may be sent and summed in bfloat16 or wider, within the bound.
No kernel may reach another device: no remote copies, remote signals or barrier semaphores. Data moves between devices by JAX's collectives and lax.ppermute only.
A program may use at most 128 MiB of HBM per device.

v0:
```python
import jax
import jax.numpy as jnp
from jax import lax
from jax.sharding import PartitionSpec as P

EPS = 1e-06


def combined_all(value, axis, join):
    pieces = jax.tree.map(lambda part: lax.all_gather(part, axis), value)
    head = jax.tree.map(lambda part: part[0], pieces)
    tail = jax.tree.map(lambda part: part[1:], pieces)
    so_far, _ = lax.scan(lambda so_far, piece: (join(so_far, piece), None), head, tail)
    return so_far


def normalize(states, gain):
    values = states.astype(jnp.float32)
    scale_inv = lax.rsqrt(jnp.mean(values * values, axis=-1, keepdims=True) + EPS)
    return (values * scale_inv * gain[None, :]).astype(jnp.bfloat16)


def combine(left_part, right_part):
    highest = jnp.maximum(left_part[0], right_part[0])
    left_scale = jnp.exp(left_part[0] - highest)
    right_scale = jnp.exp(right_part[0] - highest)
    return (
        highest,
        left_part[1] * left_scale + right_part[1] * right_scale,
        left_part[2] * left_scale + right_part[2] * right_scale,
        left_part[3] + right_part[3],
    )


def score(states, wanted, gain, head):
    normed = normalize(states, gain)
    logits = jnp.einsum(
        "nd,vd->nv",
        normed,
        lax.all_gather(head, "tok", axis=0, tiled=True),
        preferred_element_type=jnp.float32,
    )
    vocab_block = head.shape[0]
    vocab_shards = lax.axis_size("vocab")
    shard_index = lax.axis_index("vocab")
    owned = wanted // vocab_block % vocab_shards == shard_index
    column = wanted // (vocab_block * vocab_shards) * vocab_block + wanted % vocab_block
    column = jnp.where(owned, column, -1)
    columns = lax.broadcasted_iota(jnp.int32, logits.shape, 1)
    highest = jnp.max(logits, axis=1)
    exponent = jnp.exp(logits - highest[:, None])
    exp_total = jnp.sum(exponent, axis=1)
    moment = jnp.sum(exponent * logits, axis=1)
    picked = jnp.sum(jnp.where(columns == column[:, None], logits, 0.0), axis=1)
    highest, exp_total, moment, picked = combined_all(
        (highest, exp_total, moment, picked), "vocab", combine
    )
    log_total = highest + jnp.log(exp_total)
    return (picked - log_total, log_total - moment / exp_total)


def on_device(hidden, gain, head, targets, lengths, group_map):
    capacity = hidden.shape[0]
    own_load = jnp.sum(lengths)
    slot_index = jnp.arange(capacity, dtype=jnp.int32)
    logprob, entropy = score(hidden, targets, gain, head)
    is_live = slot_index < own_load
    logprob = jnp.where(is_live, logprob, 0.0)
    entropy = jnp.where(is_live, entropy, 0.0)
    finish = jnp.cumsum(lengths)
    starts = finish - lengths
    member = (
        (slot_index[:, None] >= starts[None, :]) & (slot_index[:, None] < finish[None, :])
    ).astype(jnp.float32)
    request_sums = jnp.sum(member * logprob[:, None], axis=0)
    mean_logprob = request_sums / lengths.astype(jnp.float32)
    groups_count = lengths.shape[0] * lax.axis_size("tok") // 8
    onehot = (
        group_map[:, 0][:, None] == jnp.arange(groups_count, dtype=jnp.int32)[None, :]
    ).astype(jnp.float32)
    group_sums, counts = lax.psum(
        (jnp.sum(onehot * mean_logprob[:, None], axis=0), jnp.sum(onehot, axis=0)), "tok"
    )
    group_mean = group_sums / counts
    centered = mean_logprob - jnp.sum(onehot * group_mean[None, :], axis=1)
    vocab_shards = lax.axis_size("vocab")
    shard_index = lax.axis_index("vocab")
    slot_share = capacity // vocab_shards
    request_share = lengths.shape[0] // vocab_shards
    return (
        lax.dynamic_slice_in_dim(logprob, shard_index * slot_share, slot_share, 0),
        lax.dynamic_slice_in_dim(entropy, shard_index * slot_share, slot_share, 0),
        lax.dynamic_slice_in_dim(centered, shard_index * request_share, request_share, 0),
    )


def solution(mesh):
    return jax.shard_map(
        on_device,
        mesh=mesh,
        in_specs=(
            P("tok", None),
            P(),
            P(("tok", "vocab"), None),
            P("tok"),
            P("tok"),
            P("tok", None),
        ),
        out_specs=(P(("tok", "vocab")), P(("tok", "vocab")), P(("tok", "vocab"))),
        check_vma=False,
    )
```

profile of v0, /device:TPU:0, one launch (start us, length us, event | category | flops | bytes accessed | tf_op | source)
XLA Modules:
  0.0 337.3 jit_solution(6766932386093546986)
XLA Ops:
  7.2 0.0 all-gather.10.cloned.1.call-start
  7.2 0.7 all-gather.10.cloned.1.call-update
  7.9 0.8 reduce-window.8
  8.7 1.3 bitcast_subtract_fusion
  10.0 0.7 iota_compare_fusion.3
  10.7 4.1 %fusion.1 = f32[1536]{0:T(1024)S(1)} fusion(bf16[1536,2048]{1,0:T(8,128)(2,1)} %param.8), kind=kLoop, calls=%fused_computation.15 | loop fusion | flops 9435648 | bytes 6297600 | tf_op jit(solution)/shard_map/reduce_sum | solution.py:19
  14.8 0.7 fusion.14
  15.5 225.0 %all-gather.10.cloned.1.call-done = bf16[4096,2048]{1,0:T(8,128)(2,1)} async-done(((bf16[512,2048]{1,0:T(8,128)(2,1)}), bf16[4096,2048]{1,0:T(8,128)(2,1)}) %all-gather.10.cloned.1.call-update) | async-done | bytes 16777232 | tf_op jit(solution)/shard_map/all_gather | solution.py:40
  240.5 34.0 %fusion.20 = (f32[1536]{0:T(1024)S(1)}, f32[1536,4096]{1,0:T(8,128)}) fusion(bf16[4096,2048]{1,0:T(8,128)(2,1)} %all-gather.10.cloned.1.call-done, bf16[1536,2048]{1,0:T(8,128)(2,1)} %param.8, f32[2048]{0:T(1024)} %param.9, f32[1536]{0:T(1024)S(1)} %add_rsqrt_fusion), kind=kOutput, calls=%fused_computation.68 | convolution fusion | flops 25788676096 | bytes 48254976 | tf_op jit(solution)/shard_map/nd,vd->nv/dot_general | solution.py:37
  274.4 0.0 copy-start
  274.4 0.0 copy-start.1
  274.4 13.0 %multiply_reduce_fusion = (f32[1536]{0:T(1024)S(1)}, f32[1536]{0:T(1024)S(1)}, f32[1536]{0:T(1024)S(1)}) fusion(f32[1536,4096]{1,0:T(8,128)} %get-tuple-element.93, f32[1536]{0:T(1024)S(1)} %get-tuple-element.92, s32[1536]{0:T(1024)S(1)} %fusion.14), kind=kLoop, calls=%fused_computation.10 | loop fusion | flops 44035584 | bytes 25196544 | tf_op jit(solution)/shard_map/reduce_sum | solution.py:53
  287.4 5.2 %all-gather.7 = f32[4,1,1536]{2,1,0:T(1,128)S(1)} all-gather(f32[1,1,1536]{2,1,0:T(1,128)S(1)} %reshape.68), channel_id=5, replica_groups=mesh['tok'=8,'vocab'=4] {'vocab'}, dimensions={0}, use_global_device_ids=true | all-gather | bytes 30720 | tf_op jit(solution)/shard_map/all_gather | solution.py:10
  292.7 5.2 %all-gather.6 = f32[4,1,1536]{2,1,0:T(1,128)S(1)} all-gather(f32[1,1,1536]{2,1,0:T(1,128)S(1)} %reshape.66), channel_id=4, replica_groups=mesh['tok'=8,'vocab'=4] {'vocab'}, dimensions={0}, use_global_device_ids=true | all-gather | bytes 30720 | tf_op jit(solution)/shard_map/all_gather | solution.py:10
  297.9 5.2 %all-gather.5 = f32[4,1,1536]{2,1,0:T(1,128)S(1)} all-gather(f32[1,1,1536]{2,1,0:T(1,128)S(1)} %reshape.64), channel_id=3, replica_groups=mesh['tok'=8,'vocab'=4] {'vocab'}, dimensions={0}, use_global_device_ids=true | all-gather | bytes 30720 | tf_op jit(solution)/shard_map/all_gather | solution.py:10
  303.1 5.2 %all-gather.4 = f32[4,1,1536]{2,1,0:T(1,128)S(1)} all-gather(f32[1,1,1536]{2,1,0:T(1,128)S(1)} %reshape.62), channel_id=2, replica_groups=mesh['tok'=8,'vocab'=4] {'vocab'}, dimensions={0}, use_global_device_ids=true | all-gather | bytes 30720 | tf_op jit(solution)/shard_map/all_gather | solution.py:10
  308.4 0.5 while.16
  309.0 0.7 subtract_select_fusion
  309.6 0.2 select_reduce_fusion.1
  309.8 0.0 copy-done
  309.8 0.0 copy-done.1
  309.8 0.1 convert_reduce_fusion
  309.9 18.4 %all-reduce = (f32[8]{0:T(128)S(1)}, f32[8]{0:T(128)S(1)}) all-reduce(f32[8]{0:T(128)S(1)} %get-tuple-element.61, f32[8]{0:T(128)S(1)} %get-tuple-element.60), channel_id=1, replica_groups=mesh['tok'=8,'vocab'=4] {'tok'}, use_global_device_ids=true, to_apply=%region_11.12 | all-reduce | flops 16 | bytes 128 | tf_op jit(solution)/shard_map/psum | solution.py:81
  328.4 0.2 select_reduce_fusion.2
  328.6 0.7 dynamic_slice.22
  329.2 0.6 dynamic_slice.24
  329.8 0.7 fusion.19
  (38 shorter events, 0.5 us)
Async XLA Ops:
  7.2 233.3 %all-gather.10.cloned.1.call-start = ((), (), s32[]{:S(2)}) async-start(), calls=%async_computation | async-start | bytes 18874368 | tf_op jit(solution)/shard_map/all_gather | solution.py:40
  274.4 35.4 %copy-start = (s32[8]{0:T(128)S(1)}, s32[8]{0:T(128)}, u32[]{:S(2)}) copy-start(s32[8]{0:T(128)} %param.12) | copy-start | bytes 100
  274.4 35.4 %copy-start.1 = (s32[8,1]{0,1:T(1,128)S(1)}, s32[8,1]{0,1:T(1,128)}, u32[]{:S(2)}) copy-start(s32[8,1]{0,1:T(1,128)} %param.13) | copy-start | bytes 100
Sparse Core Ops, SparseCore 0:
  10.1 230.2 all-gather.9
where the time goes:
time: 338 us; the launch traced here: 337 us
  waiting for transfers between devices  226 us (67%)
  blocking collectives  39.2 us (12%)
  matrix products  34 us (10%)
  other arithmetic  22.5 us (7%)
  between operations  14.2 us (4%)
    all_gather x1, waiting for transfers between devices, score(): lax.all_gather(head, 'tok', axis=0, tiled=True)  225 us
    dot_general x1, matrix products, score(): jnp.einsum('nd,vd->nv', normed, lax.all_gather(head, 'tok', axis=0, tiled...  34 us
    all_gather x4, blocking collectives, combined_all(): pieces = jax.tree.map(lambda part: lax.all_gather(part, axis), value)  20.8 us
    psum x1, blocking collectives, on_device(): lax.psum((jnp.sum(onehot * mean_logprob[:, None], axis=0), jnp.sum(onehot...  18.4 us
    reduce_sum x1, other arithmetic, score(): moment = jnp.sum(exponent * logits, axis=1)  13 us
  transfers between devices with their start and end apart: 1, of which 1 were waited for; matrix products, arithmetic and copies ran while one was open for 2% of the time, Pallas kernels for 0%

commit v1 on v0

--- a/solution.py
+++ b/solution.py
@@ -1,9 +1,16 @@
+import functools
+
 import jax
 import jax.numpy as jnp
 from jax import lax
+from jax.experimental import pallas as pl
+from jax.experimental.pallas import tpu as pltpu
 from jax.sharding import PartitionSpec as P
 
 EPS = 1e-06
+LOW = -1e30
+BOTH = ("tok", "vocab")
+TOK, VOCAB, NZ, NY = 8, 4, 4, 2
 
 
 def combined_all(value, axis, join):
@@ -17,7 +24,7 @@
 def normalize(states, gain):
     values = states.astype(jnp.float32)
     scale_inv = lax.rsqrt(jnp.mean(values * values, axis=-1, keepdims=True) + EPS)
-    return (values * scale_inv * gain[None, :]).astype(jnp.bfloat16)
+    return (values * scale_inv * gain).astype(jnp.bfloat16)
 
 
 def combine(left_part, right_part):
@@ -33,7 +40,7 @@
 
 
 def score(states, wanted, gain, head):
-    normed = normalize(states, gain)
+    normed = normalize(states, gain[None, :])
     logits = jnp.einsum(
         "nd,vd->nv",
         normed,
@@ -59,7 +66,7 @@
     return (picked - log_total, log_total - moment / exp_total)
 
 
-def on_device(hidden, gain, head, targets, lengths, group_map):
+def on_any_mesh(hidden, gain, head, targets, lengths, group_map):
     capacity = hidden.shape[0]
     own_load = jnp.sum(lengths)
     slot_index = jnp.arange(capacity, dtype=jnp.int32)
@@ -94,9 +101,417 @@
     )
 
 
+def device_pairs(target):
+    pairs = []
+    for z in range(NZ):
+        for y in range(NY):
+            for x in range(2):
+                for c in range(2):
+                    to = target(z, y, x, c)
+                    if to is not None:
+                        pairs.append(
+                            ((z * NY + y) * VOCAB + x * 2 + c, (to[0] * NY + to[1]) * VOCAB + to[2] * 2 + to[3])
+                        )
+    return pairs
+
+
+def send(value, target):
+    return lax.ppermute(value, BOTH, device_pairs(target))
+
+
+def to_x(value):
+    return send(value, lambda z, y, x, c: (z, y, 1 - x, c))
+
+
+def to_y(value):
+    return send(value, lambda z, y, x, c: (z, 1 - y, x, c))
+
+
+def to_core(value):
+    return send(value, lambda z, y, x, c: (z, y, x, 1 - c))
+
+
+def to_partner(value):
+    return send(value, lambda z, y, x, c: (z ^ 2, y, x, c))
+
+
+def round_z(value, step):
+    return send(value, lambda z, y, x, c: ((z + step) % NZ, y, x, c))
+
+
+def up(value, first):
+    return send(value, lambda z, y, x, c: (z + 1, y, x, c) if first <= z < NZ - 1 else None)
+
+
+def down(value, first):
+    return send(value, lambda z, y, x, c: (z - 1, y, x, c) if 0 < z <= NZ - 1 - first else None)
+
+
+SHARE = 384
+EVEN = 240
+SURE = 96
+REST = EVEN - SURE
+PIECE = 256
+
+
+def prep_kernel(which, h0, h1, h2, h3, gain_ref, sure_ref, rest_ref, trade_ref):
+    gain = gain_ref[...]
+    row = lax.broadcasted_iota(jnp.int32, (SURE, SURE), 0)
+    col = lax.broadcasted_iota(jnp.int32, (SURE, SURE), 1)
+    mirror = (row + col == SURE - 1).astype(jnp.bfloat16)
+
+    def flip(block):
+        return jnp.dot(mirror, block, preferred_element_type=jnp.float32).astype(jnp.bfloat16)
+
+    sure_ref[...] = normalize(h0[...], gain)
+    rest_ref[0:SURE, :] = normalize(h1[...], gain)
+    third = normalize(h2[...], gain)
+    rest_ref[SURE:REST, :] = third[0 : REST - SURE, :]
+    trade_ref[0:SURE, :] = flip(normalize(h3[...], gain))
+    trade_ref[SURE:REST, :] = flip(third)[0 : REST - SURE, :]
+
+
+def prepare(hidden, gain, quarter):
+    width = hidden.shape[1]
+
+    def block(j):
+        return pl.BlockSpec((SURE, width), lambda i, which, j=j: (VOCAB * j + which[0], 0))
+
+    def whole(rows):
+        return pl.BlockSpec((rows, width), lambda i, which: (0, 0))
+
+    return pl.pallas_call(
+        prep_kernel,
+        grid_spec=pltpu.PrefetchScalarGridSpec(
+            num_scalar_prefetch=1,
+            grid=(1,),
+            in_specs=[block(j) for j in range(4)] + [whole(1)],
+            out_specs=[whole(SURE), whole(REST), whole(REST)],
+        ),
+        out_shape=[jax.ShapeDtypeStruct((n, width), jnp.bfloat16) for n in (SURE, REST, REST)],
+        cost_estimate=pl.CostEstimate(flops=4 * 10**8, bytes_accessed=3 * 10**6, transcendentals=SHARE),
+        name="prep",
+    )(quarter.reshape(1), hidden, hidden, hidden, hidden, gain[None, :])
+
+
+def stats_kernel(plan, n_pieces, n_tok_refs, head_plan, scalars, tgt_ref, *refs):
+    tok_refs = refs[:n_tok_refs]
+    n_head_refs = 1 + max(index for index, _ in head_plan)
+    head_refs = refs[n_tok_refs : n_tok_refs + n_head_refs]
+    out_ref, tok_buf, head_buf, logit_buf, state, tok_sem, head_sem = refs[n_tok_refs + n_head_refs :]
+    tokens = tok_buf.shape[0]
+    z = scalars[0]
+    for piece, (index, start) in enumerate(head_plan):
+        pltpu.make_async_copy(
+            head_refs[index].at[pl.ds(start, PIECE)],
+            head_buf.at[pl.ds(piece * PIECE, PIECE)],
+            head_sem.at[piece],
+        ).start()
+    for at in range(NZ):
+
+        @pl.when(z == at)
+        def _():
+            for seg, (index, offset) in enumerate(plan[at]):
+                ref = tok_refs[index]
+                pltpu.make_async_copy(
+                    ref, tok_buf.at[pl.ds(offset, ref.shape[0])], tok_sem.at[seg]
+                ).start()
+
+    for seg, (index, offset) in enumerate(plan[0]):
+        ref = tok_refs[index]
+        pltpu.make_async_copy(ref, tok_buf.at[pl.ds(offset, ref.shape[0])], tok_sem.at[seg]).wait()
+    state[0] = jnp.full((8, tokens), LOW, jnp.float32)
+    for k in range(1, 4):
+        state[k] = jnp.zeros((8, tokens), jnp.float32)
+    group = 2 * PIECE
+    chunk = 32 if tokens > 300 else 64
+
+    def part(row):
+        return logit_buf[row : row + chunk, :].reshape(chunk // 8, 8, tokens)
+
+    rows = lax.broadcasted_iota(jnp.int32, (chunk // 8, 8, tokens), 0) * 8 + lax.broadcasted_iota(
+        jnp.int32, (chunk // 8, 8, tokens), 1
+    )
+
+    def body(g, carry):
+        for half in range(2):
+            pltpu.make_async_copy(
+                head_refs[0].at[pl.ds(0, PIECE)],
+                head_buf.at[pl.ds(g * group + half * PIECE, PIECE)],
+                head_sem.at[2 * g + half],
+            ).wait()
+        logit_buf[...] = lax.dot_general(
+            head_buf[pl.ds(g * group, group), :],
+            tok_buf[...],
+            (((1,), (1,)), ((), ())),
+            preferred_element_type=jnp.float32,
+        )
+        top_before = state[0]
+        top = top_before
+        for row in range(0, group, chunk):
+            top = jnp.maximum(top, jnp.max(part(row), axis=0))
+        shift = top_before - top
+        scale = jnp.exp(shift)
+        total = state[1] * scale
+        moment = (state[2] + shift * state[1]) * scale
+        picked = state[3]
+        for half in range(2):
+            wanted = tgt_ref[...] - scalars[1 + 2 * g + half]
+            for row in range(0, PIECE, chunk):
+                logits = part(half * PIECE + row)
+                under = logits - top[None]
+                weight = jnp.exp(under)
+                total += jnp.sum(weight, axis=0)
+                moment += jnp.sum(weight * under, axis=0)
+                picked += jnp.sum(
+                    jnp.where(rows == (wanted - row)[None], logits, 0.0), axis=0
+                )
+        state[0] = top
+        state[1] = total
+        state[2] = moment
+        state[3] = picked
+        return carry
+
+    lax.fori_loop(0, n_pieces // 2, body, 0)
+    top8 = state[0]
+    top = jnp.max(top8, axis=0, keepdims=True)
+    shift = top8 - top
+    scale = jnp.exp(shift)
+    out_ref[0:1, :] = top
+    out_ref[1:2, :] = jnp.sum(state[1] * scale, axis=0, keepdims=True)
+    out_ref[2:3, :] = jnp.sum((state[2] + shift * state[1]) * scale, axis=0, keepdims=True)
+    out_ref[3:4, :] = jnp.sum(state[3], axis=0, keepdims=True)
+    out_ref[4:8, :] = jnp.zeros((4, tokens), jnp.float32)
+
+
+def statistics(name, z, wanted, tok_refs, plan, heads):
+    tokens = wanted.shape[1]
+    arrays, head_plan = [], []
+    for array, start, _ in heads:
+        for index, known in enumerate(arrays):
+            if known is array:
+                break
+        else:
+            index = len(arrays)
+            arrays.append(array)
+        head_plan.append((index, start))
+    scalars = jnp.stack([z] + [base for _, _, base in heads]).astype(jnp.int32)
+    width = arrays[0].shape[1]
+    n_pieces = len(heads)
+    vocab = n_pieces * PIECE
+    return pl.pallas_call(
+        functools.partial(stats_kernel, plan, n_pieces, len(tok_refs), head_plan),
+        grid_spec=pltpu.PrefetchScalarGridSpec(
+            num_scalar_prefetch=1,
+            grid=(1,),
+            in_specs=[pl.BlockSpec((1, tokens), lambda i, s: (0, 0))]
+            + [pl.BlockSpec(memory_space=pl.ANY)] * (len(tok_refs) + len(arrays)),
+            out_specs=pl.BlockSpec((8, tokens), lambda i, s: (0, 0)),
+            scratch_shapes=[
+                pltpu.VMEM((tokens, width), jnp.bfloat16),
+                pltpu.VMEM((vocab, width), jnp.bfloat16),
+                pltpu.VMEM((2 * PIECE, tokens), jnp.float32),
+                pltpu.VMEM((4, 8, tokens), jnp.float32),
+                pltpu.SemaphoreType.DMA((len(plan[0]),)),
+                pltpu.SemaphoreType.DMA((n_pieces,)),
+            ],
+        ),
+        out_shape=jax.ShapeDtypeStruct((8, tokens), jnp.float32),
+        compiler_params=pltpu.CompilerParams(vmem_limit_bytes=32 * 1024 * 1024),
+        cost_estimate=pl.CostEstimate(
+            flops=2 * tokens * vocab * width,
+            bytes_accessed=2 * (tokens + vocab) * width,
+            transcendentals=tokens * vocab,
+        ),
+        name=name,
+    )(scalars, wanted, *tok_refs, *arrays)
+
+
+def join(parts):
+    top = functools.reduce(jnp.maximum, [part[0] for part in parts])
+    total = moment = picked = 0.0
+    for part in parts:
+        shift = part[0] - top
+        scale = jnp.exp(shift)
+        total += part[1] * scale
+        moment += (part[2] + shift * part[1]) * scale
+        picked += part[3]
+    return top, total, moment, picked
+
+
+def on_device(hidden, gain, head, targets, lengths, group_map):
+    tok = lax.axis_index("tok")
+    vocab = lax.axis_index("vocab")
+    z, y = tok // NY, tok % NY
+    x, core = vocab // 2, vocab % 2
+    upper = z >= NZ // 2
+    quarter = jnp.where(upper, VOCAB - 1 - vocab, vocab)
+
+    sure, rest_own, trade = prepare(hidden, gain, quarter)
+    traded = to_partner(trade)
+    load = jnp.sum(lengths)
+    block_start = (jnp.arange(4) * VOCAB + quarter) * SURE
+    live = jnp.sum(jnp.clip(load - block_start, 0, SURE))
+    slot = lax.broadcasted_iota(jnp.int32, (REST, 1), 0) + SURE
+    rest = jnp.where(slot < live, rest_own, traded)
+
+    def line(value):
+        ups, downs = [value], [value]
+        for first in range(NZ - 1):
+            ups.append(up(ups[-1], first))
+            downs.append(down(downs[-1], first))
+        return ups, downs
+
+    sure_up, sure_down = line(sure)
+    rest_up, rest_down = line(rest)
+
+    own_small = jnp.concatenate(
+        [
+            lax.dynamic_index_in_dim(targets.reshape(4, VOCAB, SURE), quarter, 1, False).reshape(-1),
+            lengths,
+            group_map[:, 0],
+            jnp.zeros((112,), jnp.int32),
+        ]
+    )
+    turned = jnp.stack([own_small] + [round_z(own_small, step) for step in (1, 2, 3)])
+    source = (z - jnp.arange(NZ)) % NZ
+    small = jnp.sum(
+        jnp.where((source[None, :] == jnp.arange(NZ)[:, None])[:, :, None], turned[None], 0), axis=1
+    )
+    tgt = small[:, :SHARE]
+    meta_own = small[:, SHARE : SHARE + 16]
+    meta_other = to_y(meta_own)
+    meta = jnp.where(y == 0, jnp.stack([meta_own, meta_other], 1), jnp.stack([meta_other, meta_own], 1))
+    all_lengths, all_groups = meta[:, :, :8], meta[:, :, 8:]
+
+    zs = jnp.arange(NZ)
+    loads = jnp.sum(meta_own[:, :8], axis=1)
+    quarters = jnp.where(zs >= NZ // 2, VOCAB - 1 - vocab, vocab)
+    starts_of = (jnp.arange(4)[None, :] * VOCAB + quarters[:, None]) * SURE
+    lives = jnp.sum(jnp.clip(loads[:, None] - starts_of, 0, SURE), axis=1)
+    slots = jnp.arange(EVEN)
+    stays = slots[None, :] < lives[:, None]
+    partner = jnp.array([2, 3, 0, 1])
+    tgt_back = jnp.flip(jnp.concatenate([tgt[2:], tgt[:2]], 0)[:, SHARE - REST :], 1)
+    tgt_even = jnp.where(
+        stays, tgt[:, :EVEN], jnp.concatenate([tgt[:, :SURE], tgt_back], 1)
+    ) - z * (TOK * VOCAB // NZ * head.shape[0])
+    tgt_sure = tgt_even[:, :SURE].reshape(1, NZ * SURE)
+    tgt_rest = tgt_even[:, SURE:]
+    tgt_near = jnp.where(upper, tgt_rest[2:], tgt_rest[:2]).reshape(1, 2 * REST)
+    tgt_mid = jnp.where(upper, tgt_rest[1:2], tgt_rest[2:3])
+    tgt_far = jnp.where(upper, tgt_rest[0:1], tgt_rest[3:4])
+
+    low_half, high_half = head[:PIECE], head[PIECE:]
+    xa, ya = to_x(low_half), to_y(high_half)
+    xb, yb = to_x(high_half), to_y(low_half)
+    x2, y2 = to_x(ya), to_y(xa)
+
+    def base(at_y, at_x, at_core, half):
+        return ((at_y * 2 + at_x) * 2 + at_core) * (2 * PIECE) + half * PIECE
+
+    def both_cores(piece, at_y, at_x, half):
+        return [
+            (piece, 0, base(at_y, at_x, core, half)),
+            (to_core(piece), 0, base(at_y, at_x, 1 - core, half)),
+        ]
+
+    head_core = to_core(head)
+    heads_own = [
+        (array, half * PIECE, base(y, x, at_core, half))
+        for array, at_core in ((head, core), (head_core, 1 - core))
+        for half in range(2)
+    ]
+    heads_a = heads_own + both_cores(xa, y, 1 - x, 0) + both_cores(ya, 1 - y, x, 1)
+    heads_b = both_cores(xb, y, 1 - x, 1) + both_cores(yb, 1 - y, x, 0)
+    heads_c = both_cores(x2, 1 - y, 1 - x, 1) + both_cores(y2, 1 - y, 1 - x, 0)
+
+    def from_set(at, of):
+        return at - of if of <= at else 3 + of - at
+
+    sure_refs = sure_up + sure_down[1:]
+    rest_refs = rest_up + rest_down[1:]
+    plan_sure = [[(from_set(at, of), of * SURE) for of in range(NZ)] for at in range(NZ)]
+    plan_near = [[(from_set(at, at // 2 * 2 + k), k * REST) for k in range(2)] for at in range(NZ)]
+    plan_mid = [[(from_set(at, 2 if at < 2 else 1), 0)] for at in range(NZ)]
+    plan_far = [[(from_set(at, 3 if at < 2 else 0), 0)] for at in range(NZ)]
+
+    def compact(refs, plan):
+        used = sorted({index for rows in plan for index, _ in rows})
+        return [refs[index] for index in used], [
+            [(used.index(index), offset) for index, offset in rows] for rows in plan
+        ]
+
+    near_refs, plan_near = compact(rest_refs, plan_near)
+    mid_refs, plan_mid = compact(rest_refs, plan_mid)
+    far_refs, plan_far = compact(rest_refs, plan_far)
+    sure_1 = statistics("sure_ab", z, tgt_sure, sure_refs, plan_sure, heads_a + heads_b)
+    near_1 = statistics("near_ab", z, tgt_near, near_refs, plan_near, heads_a + heads_b)
+    plan_c = [
+        a + [(index + len(sure_refs), offset + NZ * SURE) for index, offset in b]
+        for a, b in zip(plan_sure, plan_near)
+    ]
+    both_2 = statistics(
+        "early_c", z, jnp.concatenate([tgt_sure, tgt_near], 1), sure_refs + near_refs, plan_c, heads_c
+    )
+    mid = statistics("mid", z, tgt_mid, mid_refs, plan_mid, heads_a + heads_b + heads_c)
+    far = statistics("far", z, tgt_far, far_refs, plan_far, heads_a + heads_b + heads_c)
+
+    sure_all = jnp.stack(join([sure_1, both_2[:, : NZ * SURE]])).reshape(4, NZ, SURE)
+    near_all = jnp.stack(join([near_1, both_2[:, NZ * SURE :]])).reshape(4, 2, REST)
+    mid, far = mid[:4, None], far[:4, None]
+    rest_all = jnp.where(
+        upper,
+        jnp.concatenate([far, mid, near_all], 1),
+        jnp.concatenate([near_all, mid, far], 1),
+    )
+    own_stats = jnp.concatenate([sure_all, rest_all], 2)
+    top, total, moment, picked = join([own_stats] + [round_z(own_stats, step) for step in (1, 2, 3)])
+    spread = jnp.log(total)
+    logprob = picked - top - spread
+    entropy = spread - moment / total
+
+    local = jnp.where(stays, slots[None, :], 2 * EVEN - 1 - slots[None, :])
+    origin = jnp.where(stays, zs[:, None], partner[:, None])
+    origin_quarter = jnp.where(origin >= NZ // 2, VOCAB - 1 - vocab, vocab)
+    row = (local // SURE * VOCAB + origin_quarter) * SURE + local % SURE
+    place = origin * hidden.shape[0] + row
+    finish = jnp.cumsum(meta_own[:, :8], axis=1) + zs[:, None] * hidden.shape[0]
+    begin = finish - meta_own[:, :8]
+    member = (place[:, :, None, None] >= begin) & (place[:, :, None, None] < finish)
+    sums_part = jnp.sum(jnp.where(member, logprob[:, :, None, None], 0.0), axis=(0, 1))
+
+    results = jnp.stack([logprob, entropy])
+    mine = lax.dynamic_index_in_dim(results, z, 1, False)
+    theirs = lax.dynamic_index_in_dim(results, z ^ 2, 1, False)
+    local_rows = jnp.concatenate([mine, jnp.flip(theirs[:, SURE:], 1)], 1)
+    local_rows = jnp.where(jnp.arange(SHARE)[None, :] < live, local_rows, 0.0)
+    gathered = lax.all_gather(
+        jnp.concatenate([local_rows.reshape(1, -1), sums_part.reshape(1, -1)], 1), "vocab"
+    ).reshape(VOCAB, -1)
+    sums_own = jnp.sum(gathered[:, 2 * SHARE :], axis=0)
+    sums_other = to_y(sums_own)
+    sums = jnp.where(
+        y == 0, jnp.stack([sums_own, sums_other]), jnp.stack([sums_other, sums_own])
+    ).reshape(NY, NZ, 8).transpose(1, 0, 2)
+    parts = gathered[:, : 2 * SHARE].reshape(VOCAB, 2, SHARE)
+    parts = lax.dynamic_slice_in_dim(parts, vocab * SURE, SURE, 2)
+    parts = jnp.where(upper, jnp.flip(parts, 0), parts)
+    out = parts.transpose(1, 0, 2).reshape(2, SHARE)
+
+    means = (sums / all_lengths.astype(jnp.float32)).reshape(-1)
+    onehot = (
+        all_groups.reshape(-1)[:, None] == jnp.arange(TOK, dtype=jnp.int32)[None, :]
+    ).astype(jnp.float32)
+    group_mean = jnp.sum(onehot * means[:, None], axis=0) / jnp.sum(onehot, axis=0)
+    centered = means - jnp.sum(onehot * group_mean[None, :], axis=1)
+    return out[0], out[1], lax.dynamic_slice_in_dim(centered, tok * 8 + vocab * 2, 2, 0)
+
+
 def solution(mesh):
+    fits = mesh.shape["tok"] == TOK and mesh.shape["vocab"] == VOCAB
     return jax.shard_map(
-        on_device,
+        on_device if fits else on_any_mesh,
         mesh=mesh,
         in_specs=(
             P("tok", None),

time: 338 us -> 238 us (0.70)
  waiting for transfers between devices: 226 us -> 83 us
  Pallas kernels: 0 us -> 61.1 us
  starting transfers between devices: 0.04 us -> 55.9 us
  blocking collectives: 39.2 us -> 5.17 us
  matrix products: 34 us -> 0 us
  local copies, waits for them, and re-layouts: 1.66 us -> 19 us
  between operations: 14.2 us -> 1.24 us
  other arithmetic: 22.5 us -> 12 us
    all_gather x1 -> x0, waiting for transfers between devices: 225 us -> none  [score(): lax.all_gather(head, 'tok', axis=0, tiled=True)]
    ppermute x0 -> x34, waiting for transfers between devices: none -> 83 us  [send(): return lax.ppermute(value, BOTH, device_pairs(target))]
    pallas_call x0 -> x6, Pallas kernels: none -> 61.1 us  [the longest x5 57.8 us: statistics(): pl.pallas_call(functools.partial(stats_kernel, plan, n_pieces, len(tok_re...]
    ppermute x0 -> x34, starting transfers between devices: none -> 55.9 us  [send(): return lax.ppermute(value, BOTH, device_pairs(target))]
    dot_general x1 -> x0, matrix products: 34 us -> none  [score(): jnp.einsum('nd,vd->nv', normed, lax.all_gather(head, 'tok', axis=0, tiled...]
    psum x1 -> x0, blocking collectives: 18.4 us -> none  [on_device(): lax.psum((jnp.sum(onehot * mean_logprob[:, None], axis=0), jnp.sum(onehot...]
    all_gather x4 -> x1, blocking collectives: 20.8 us -> 5.17 us  [on_device(): lax.all_gather(jnp.concatenate([local_rows.reshape(1, -1), sums_part.resh...]
    reduce_sum x4 -> x7, other arithmetic: 17.4 us -> 3.88 us  [the longest x1 1.36 us: on_device(): load = jnp.sum(lengths)]
  transfers between devices with their start and end apart: 1 -> 34, of which waited for: 1 -> 10; matrix products, arithmetic and copies ran while one was open for 2% -> 7% of each run, Pallas kernels for 0% -> 24%
where the time goes in v1:
time: 238 us; the launch traced here: 237 us
  waiting for transfers between devices  83 us (35%)
  Pallas kernels  61.1 us (26%)
  starting transfers between devices  55.9 us (23%)
  local copies, waits for them, and re-layouts  19 us (8%)
  other arithmetic  12 us (5%)
  blocking collectives  5.17 us (2%)
    ppermute x34, waiting for transfers between devices, send(): return lax.ppermute(value, BOTH, device_pairs(target))  83 us
    pallas_call x5, Pallas kernels, statistics(): pl.pallas_call(functools.partial(stats_kernel, plan, n_pieces, len(tok_re...  57.8 us
    ppermute x34, starting transfers between devices, send(): return lax.ppermute(value, BOTH, device_pairs(target))  55.9 us
    unnamed x65, local copies, waits for them, and re-layouts  13.6 us
    all_gather x1, blocking collectives, on_device(): lax.all_gather(jnp.concatenate([local_rows.reshape(1, -1), sums_part.resh...  5.17 us
  transfers between devices with their start and end apart: 34, of which 10 were waited for; matrix products, arithmetic and copies ran while one was open for 7% of the time, Pallas kernels for 24%

profile of v1, /device:TPU:0, one launch (start us, length us, event | category | flops | bytes accessed | tf_op | source)
XLA Modules:
  0.0 237.3 jit_solution(16651972580150023581)
XLA Ops:
  0.7 3.3 %prep.1 = (bf16[96,2048]{1,0:T(8,128)(2,1)}, bf16[144,2048]{1,0:T(8,128)(2,1)}, bf16[144,2048]{1,0:T(8,128)(2,1)}) custom-call(s32[1]{0:T(128)} %bitcast.18.which, bf16[1536,2048]{1,0:T(8,128)(2,1)} %h3.1, bf16[1536,2048]{1,0:T(8,128)(2,1)} %h3.1, bf16[1536,2048]{1,0:T(8,128)(2,1)} %h3.1, bf16[1536,2048]{1,0:T(8,128)(2,1)} %h3.1, f32[1,2048]{1,0:T(1,128)} %bitcast.140), custom_call_target="tpu_custom_call" | custom-call | flops 400000000 | bytes 3000000 | tf_op jit(solution)/shard_map/prep/pallas_call | solution.py:183
  4.0 4.9 %collective-permute-start.3 = (bf16[96,2048]{1,0:T(8,128)(2,1)}, bf16[96,2048]{1,0:T(8,128)(2,1)S(1)}, u32[]{:S(2)}, u32[]{:S(2)}) collective-permute-start(bf16[96,2048]{1,0:T(8,128)(2,1)} %get-tuple-element.6.refs_0_), channel_id=1, source_target_pairs={{0,8},{1,9},{2,10},{3,11},{4,12},{5,13},{6,14},{7,15},{8,16},{9,17... | collective-permute-start | bytes 1179656 | tf_op jit(solution)/shard_map/ppermute | solution.py:119
  10.2 3.7 %collective-permute-start.18 = (bf16[144,2048]{1,0:T(8,128)(2,1)}, bf16[144,2048]{1,0:T(8,128)(2,1)}, u32[]{:S(2)}, u32[]{:S(2)}) collective-permute-start(bf16[144,2048]{1,0:T(8,128)(2,1)} %get-tuple-element.8), channel_id=1, source_target_pairs={{0,16},{1,17},{2,18},{3,19},{4,20},{5,21},{6,22},{7,23},{8,24},{9,... | collective-permute-start | bytes 1769480 | tf_op jit(solution)/shard_map/ppermute | solution.py:119
  15.4 1.5 collective-permute-start.10
  17.8 2.2 collective-permute-start
  20.1 16.3 %collective-permute-done = s32[512]{0:T(512)S(1)} collective-permute-done((s32[512]{0:T(512)S(1)}, s32[512]{0:T(512)S(1)}, u32[]{:S(2)}, u32[]{:S(2)}) %collective-permute-start) | collective-permute-done | bytes 2080 | tf_op jit(solution)/shard_map/ppermute | solution.py:119
  36.4 9.9 %collective-permute-start.1 = (s32[512]{0:T(512)S(1)}, s32[512]{0:T(512)S(1)}, u32[]{:S(2)}, u32[]{:S(2)}) collective-permute-start(s32[512]{0:T(512)S(1)} %pad_add_fusion.3), channel_id=1, source_target_pairs={{0,16},{1,17},{2,18},{3,19},{4,20},{5,21},{6,22},{7,23},{8,24},{9,... | collective-permute-start | bytes 6152 | tf_op jit(solution)/shard_map/ppermute | solution.py:119
  46.3 1.8 collective-permute-done.1
  48.4 3.3 %collective-permute-done.2 = s32[512]{0:T(512)S(1)} collective-permute-done((s32[512]{0:T(512)S(1)}, s32[512]{0:T(512)S(1)}, u32[]{:S(2)}, u32[]{:S(2)}) %collective-permute-start.2) | collective-permute-done | bytes 2080 | tf_op jit(solution)/shard_map/ppermute | solution.py:119
  51.6 1.5 collective-permute-start.12
  53.2 1.5 collective-permute-start.14
  62.5 10.5 %collective-permute-done.7.refs_5_ = bf16[96,2048]{1,0:T(8,128)(2,1)S(1)} collective-permute-done((bf16[96,2048]{1,0:T(8,128)(2,1)}, bf16[96,2048]{1,0:T(8,128)(2,1)S(1)}, u32[]{:S(2)}, u32[]{:S(2)}) %collective-permute-start.7) | collective-permute-done | bytes 393248 | tf_op jit(solution)/shard_map/ppermute | solution.py:119
  73.0 4.7 %collective-permute-start.19 = (bf16[144,2048]{1,0:T(8,128)(2,1)S(1)}, bf16[144,2048]{1,0:T(8,128)(2,1)}, u32[]{:S(2)}, u32[]{:S(2)}) collective-permute-start(bf16[144,2048]{1,0:T(8,128)(2,1)S(1)} %broadcast_select_fusion.refs_7_.refs_0_), channel_id=1, source_target_pairs={{0,8},{1,9},{2,10},{3,11},{4,12},{5,13},{6,14},{7,15},{8,16},{9,17... | collective-permute-start | bytes 1769480 | tf_op jit(solution)/shard_map/ppermute | solution.py:119
  83.3 13.6 %collective-permute-done.16.refs_15_.refs_12_.refs_11_ = bf16[256,2048]{1,0:T(8,128)(2,1)S(1)} collective-permute-done((bf16[256,2048]{1,0:T(8,128)(2,1)}, bf16[256,2048]{1,0:T(8,128)(2,1)S(1)}, u32[]{:S(2)}, u32[]{:S(2)}) %collective-permute-start.16) | collective-permute-done | bytes 1048608 | tf_op jit(solution)/shard_map/ppermute | solution.py:119
  99.5 1.5 collective-permute-start.25
  106.2 1.6 collective-permute-start.21
  107.7 12.7 %collective-permute-done.27.refs_2_.refs_3_ = bf16[144,2048]{1,0:T(8,128)(2,1)} collective-permute-done((bf16[144,2048]{1,0:T(8,128)(2,1)}, bf16[144,2048]{1,0:T(8,128)(2,1)}, u32[]{:S(2)}, u32[]{:S(2)}) %collective-permute-start.27) | collective-permute-done | bytes 589856 | tf_op jit(solution)/shard_map/ppermute | solution.py:119
  120.4 1.5 collective-permute-start.23
  124.1 8.0 %collective-permute-done.21.refs_10_.refs_14_ = bf16[256,2048]{1,0:T(8,128)(2,1)} collective-permute-done((bf16[256,2048]{1,0:T(8,128)(2,1)}, bf16[256,2048]{1,0:T(8,128)(2,1)}, u32[]{:S(2)}, u32[]{:S(2)}) %collective-permute-start.21) | collective-permute-done | bytes 1048608 | tf_op jit(solution)/shard_map/ppermute | solution.py:119
  132.1 13.2 %collective-permute-done.23.refs_12_.refs_16_ = bf16[256,2048]{1,0:T(8,128)(2,1)} collective-permute-done((bf16[256,2048]{1,0:T(8,128)(2,1)S(1)}, bf16[256,2048]{1,0:T(8,128)(2,1)}, u32[]{:S(2)}, u32[]{:S(2)}) %collective-permute-start.23) | collective-permute-done | bytes 1048608 | tf_op jit(solution)/shard_map/ppermute | solution.py:119
  145.4 1.6 collective-permute-start.33
  147.0 1.5 collective-permute-start.26
  156.0 13.0 %sure_ab.1 = f32[8,384]{1,0:T(8,128)S(1)} custom-call(s32[13]{0:T(128)S(1)} %stack.201.scalars, s32[1,384]{1,0:T(1,128)S(1)} %reshape.340.tgt_ref, bf16[96,2048]{1,0:T(8,128)(2,1)S(1)} %copy-done.10, bf16[96,2048]{1,0:T(8,128)(2,1)S(1)} %copy-done.12, bf16[96,2048]{1,0:T(8,128)(2,1)} %collective-permute-done.4.refs_2_, bf16[96,2048]{1,0:T(8,128)(2,1)S(1)} %copy-done.18, ...), custom_call_target="tpu_custom_call" | custom-call | flops 4831838208 | bytes 14155776 | tf_op jit(solution)/shard_map/sure_ab/pallas_call | solution.py:302
  169.0 13.2 %near_ab.1 = f32[8,288]{1,0:T(8,128)S(1)} custom-call(s32[13]{0:T(128)S(1)} %stack.201.scalars, s32[1,288]{1,0:T(1,128)S(1)} %reshape.342.tgt_ref, bf16[144,2048]{1,0:T(8,128)(2,1)S(1)} %copy-done.9, bf16[144,2048]{1,0:T(8,128)(2,1)} %collective-permute-done.19.refs_8_.refs_0_.refs_1_, bf16[144,2048]{1,0:T(8,128)(2,1)} %collective-permute-done.20.refs_9_.refs_2_, ...), custom_call_target="tpu_custom_call" | custom-call | flops 3623878656 | bytes 13762560 | tf_op jit(solution)/shard_map/near_ab/pallas_call | solution.py:302
  182.3 7.3 %early_c.1 = f32[8,672]{1,0:T(8,128)S(1)} custom-call(s32[5]{0:T(128)S(1)} %stack.211.scalars, s32[1,672]{1,0:T(1,128)S(1)} %pad_add_fusion.2.tgt_ref, bf16[96,2048]{1,0:T(8,128)(2,1)S(1)} %copy-done.10, bf16[96,2048]{1,0:T(8,128)(2,1)S(1)} %copy-done.13, bf16[96,2048]{1,0:T(8,128)(2,1)} %collective-permute-done.4.refs_2_, bf16[96,2048]{1,0:T(8,128)(2,1)S(1)} %copy-done.19, ...), custom_call_target="tpu_custom_call" | custom-call | flops 2818572288 | bytes 6946816 | tf_op jit(solution)/shard_map/early_c/pallas_call | solution.py:302
  193.7 12.1 %far.1 = f32[8,144]{1,0:T(8,128)S(1)} custom-call(s32[17]{0:T(128)S(1)} %stack.217.scalars, s32[1,144]{1,0:T(1,128)S(1)} %get-tuple-element.36.tgt_ref, bf16[144,2048]{1,0:T(8,128)(2,1)} %collective-permute-done.25.refs_0_.refs_1_, bf16[144,2048]{1,0:T(8,128)(2,1)} %collective-permute-done.26.refs_1_, ...), custom_call_target="tpu_custom_call" | custom-call | flops 2415919104 | bytes 17367040 | tf_op jit(solution)/shard_map/far/pallas_call | solution.py:302
  205.9 12.1 %mid.1 = f32[8,144]{1,0:T(8,128)S(1)} custom-call(s32[17]{0:T(128)S(1)} %stack.217.scalars, s32[1,144]{1,0:T(1,128)S(1)} %get-tuple-element.37.tgt_ref, bf16[144,2048]{1,0:T(8,128)(2,1)} %collective-permute-done.19.refs_8_.refs_0_.refs_1_, bf16[144,2048]{1,0:T(8,128)(2,1)} %collective-permute-done.25.refs_0_.refs_1_, ...), custom_call_target="tpu_custom_call" | custom-call | flops 2415919104 | bytes 17367040 | tf_op jit(solution)/shard_map/mid/pallas_call | solution.py:302
  218.6 3.5 %collective-permute-start.29 = (f32[4,4,240]{2,1,0:T(4,128)S(1)}, f32[4,4,240]{2,1,0:T(4,128)S(1)}, u32[]{:S(2)}, u32[]{:S(2)}) collective-permute-start(f32[4,4,240]{2,1,0:T(4,128)S(1)} %pad_maximum_fusion), channel_id=1, source_target_pairs={{0,8},{1,9},{2,10},{3,11},{4,12},{5,13},{6,14},{7,15},{8,16},{9,17... | collective-permute-start | bytes 46088 | tf_op jit(solution)/shard_map/ppermute | solution.py:119
  222.0 2.4 %collective-permute-start.31 = (f32[4,4,240]{2,1,0:T(4,128)S(1)}, f32[4,4,240]{2,1,0:T(4,128)S(1)}, u32[]{:S(2)}, u32[]{:S(2)}) collective-permute-start(f32[4,4,240]{2,1,0:T(4,128)S(1)} %pad_maximum_fusion), channel_id=1, source_target_pairs={{0,24},{1,25},{2,26},{3,27},{4,28},{5,29},{6,30},{7,31},{8,0},{9,1... | collective-permute-start | bytes 46088 | tf_op jit(solution)/shard_map/ppermute | solution.py:119
  224.6 2.0 collective-permute-done.30
  227.5 5.2 %all-gather.1 = f32[4,1,800]{2,1,0:T(1,128)S(1)} all-gather(f32[1,1,800]{2,1,0:T(1,128)S(1)} %maximum_bitcast_fusion), channel_id=2, replica_groups=mesh['tok'=8,'vocab'=4] {'vocab'}, dimensions={0}, use_global_device_ids=true | all-gather | bytes 16000 | tf_op jit(solution)/shard_map/all_gather | solution.py:489
  234.8 1.5 collective-permute-done.32
  (192 shorter events, 43.4 us)
Async XLA Ops:
  4.0 49.2 %collective-permute-start.3 = (bf16[96,2048]{1,0:T(8,128)(2,1)}, bf16[96,2048]{1,0:T(8,128)(2,1)S(1)}, u32[]{:S(2)}, u32[]{:S(2)}) collective-permute-start(bf16[96,2048]{1,0:T(8,128)(2,1)} %get-tuple-element.6.refs_0_), channel_id=1, source_target_pairs={{0,8},{1,9},{2,10},{3,11},{4,12},{5,13},{6,14},{7,15},{8,16},{9,17... | collective-permute-start | bytes 1179656 | tf_op jit(solution)/shard_map/ppermute | solution.py:119
  8.9 45.8 %collective-permute-start.6 = (bf16[96,2048]{1,0:T(8,128)(2,1)}, bf16[96,2048]{1,0:T(8,128)(2,1)}, u32[]{:S(2)}, u32[]{:S(2)}) collective-permute-start(bf16[96,2048]{1,0:T(8,128)(2,1)} %get-tuple-element.6.refs_0_), channel_id=1, source_target_pairs={{8,0},{9,1},{10,2},{11,3},{12,4},{13,5},{14,6},{15,7},{16,8},{17,9... | collective-permute-start | bytes 1179656 | tf_op jit(solution)/shard_map/ppermute | solution.py:119
  10.2 48.5 %collective-permute-start.18 = (bf16[144,2048]{1,0:T(8,128)(2,1)}, bf16[144,2048]{1,0:T(8,128)(2,1)}, u32[]{:S(2)}, u32[]{:S(2)}) collective-permute-start(bf16[144,2048]{1,0:T(8,128)(2,1)} %get-tuple-element.8), channel_id=1, source_target_pairs={{0,16},{1,17},{2,18},{3,19},{4,20},{5,21},{6,22},{7,23},{8,24},{9,... | collective-permute-start | bytes 1769480 | tf_op jit(solution)/shard_map/ppermute | solution.py:119
  15.4 62.3 %collective-permute-start.10 = (bf16[256,2048]{1,0:T(8,128)(2,1)}, bf16[256,2048]{1,0:T(8,128)(2,1)S(1)}, u32[]{:S(2)}, u32[]{:S(2)}) collective-permute-start(bf16[256,2048]{1,0:T(8,128)(2,1)} %get-tuple-element.27), channel_id=1, source_target_pairs={{0,2},{1,3},{2,0},{3,1},{4,6},{5,7},{6,4},{7,5},{8,10},{9,11},{10,... | collective-permute-start | bytes 3145736 | tf_op jit(solution)/shard_map/ppermute | solution.py:119
  17.8 18.5 %collective-permute-start = (s32[512]{0:T(512)S(1)}, s32[512]{0:T(512)S(1)}, u32[]{:S(2)}, u32[]{:S(2)}) collective-permute-start(s32[512]{0:T(512)S(1)} %pad_add_fusion.3), channel_id=1, source_target_pairs={{0,8},{1,9},{2,10},{3,11},{4,12},{5,13},{6,14},{7,15},{8,16},{9,17... | collective-permute-start | bytes 6152 | tf_op jit(solution)/shard_map/ppermute | solution.py:119
  36.4 11.7 %collective-permute-start.1 = (s32[512]{0:T(512)S(1)}, s32[512]{0:T(512)S(1)}, u32[]{:S(2)}, u32[]{:S(2)}) collective-permute-start(s32[512]{0:T(512)S(1)} %pad_add_fusion.3), channel_id=1, source_target_pairs={{0,16},{1,17},{2,18},{3,19},{4,20},{5,21},{6,22},{7,23},{8,24},{9,... | collective-permute-start | bytes 6152 | tf_op jit(solution)/shard_map/ppermute | solution.py:119
  51.6 28.2 %collective-permute-start.12 = (bf16[256,2048]{1,0:T(8,128)(2,1)}, bf16[256,2048]{1,0:T(8,128)(2,1)}, u32[]{:S(2)}, u32[]{:S(2)}) collective-permute-start(bf16[256,2048]{1,0:T(8,128)(2,1)} %get-tuple-element.28), channel_id=1, source_target_pairs={{0,4},{1,5},{2,6},{3,7},{4,0},{5,1},{6,2},{7,3},{8,12},{9,13},{10,... | collective-permute-start | bytes 3145736 | tf_op jit(solution)/shard_map/ppermute | solution.py:119
  53.2 27.4 %collective-permute-start.14 = (bf16[256,2048]{1,0:T(8,128)(2,1)}, bf16[256,2048]{1,0:T(8,128)(2,1)}, u32[]{:S(2)}, u32[]{:S(2)}) collective-permute-start(bf16[256,2048]{1,0:T(8,128)(2,1)} %get-tuple-element.28), channel_id=1, source_target_pairs={{0,2},{1,3},{2,0},{3,1},{4,6},{5,7},{6,4},{7,5},{8,10},{9,11},{10,... | collective-permute-start | bytes 3145736 | tf_op jit(solution)/shard_map/ppermute | solution.py:119
  54.7 5.1 %collective-permute-start.4 = (bf16[96,2048]{1,0:T(8,128)(2,1)S(1)}, bf16[96,2048]{1,0:T(8,128)(2,1)}, u32[]{:S(2)}, u32[]{:S(2)}) collective-permute-start(bf16[96,2048]{1,0:T(8,128)(2,1)S(1)} %collective-permute-done.3.refs_1_), channel_id=1, source_target_pairs={{8,16},{9,17},{10,18},{11,19},{12,20},{13,21},{14,22},{15,23},{16,... | collective-permute-start | bytes 1179656 | tf_op jit(solution)/shard_map/ppermute | solution.py:119
  58.7 38.2 %collective-permute-start.16 = (bf16[256,2048]{1,0:T(8,128)(2,1)}, bf16[256,2048]{1,0:T(8,128)(2,1)S(1)}, u32[]{:S(2)}, u32[]{:S(2)}) collective-permute-start(bf16[256,2048]{1,0:T(8,128)(2,1)} %get-tuple-element.27), channel_id=1, source_target_pairs={{0,4},{1,5},{2,6},{3,7},{4,0},{5,1},{6,2},{7,3},{8,12},{9,13},{10,... | collective-permute-start | bytes 3145736 | tf_op jit(solution)/shard_map/ppermute | solution.py:119
  59.8 13.2 %collective-permute-start.7 = (bf16[96,2048]{1,0:T(8,128)(2,1)}, bf16[96,2048]{1,0:T(8,128)(2,1)S(1)}, u32[]{:S(2)}, u32[]{:S(2)}) collective-permute-start(bf16[96,2048]{1,0:T(8,128)(2,1)} %collective-permute-done.6.refs_4_), channel_id=1, source_target_pairs={{8,0},{9,1},{10,2},{11,3},{12,4},{13,5},{14,6},{15,7},{16,8},{17,9... | collective-permute-start | bytes 1179656 | tf_op jit(solution)/shard_map/ppermute | solution.py:119
  73.0 26.5 %collective-permute-start.19 = (bf16[144,2048]{1,0:T(8,128)(2,1)S(1)}, bf16[144,2048]{1,0:T(8,128)(2,1)}, u32[]{:S(2)}, u32[]{:S(2)}) collective-permute-start(bf16[144,2048]{1,0:T(8,128)(2,1)S(1)} %broadcast_select_fusion.refs_7_.refs_0_), channel_id=1, source_target_pairs={{0,8},{1,9},{2,10},{3,11},{4,12},{5,13},{6,14},{7,15},{8,16},{9,17... | collective-permute-start | bytes 1769480 | tf_op jit(solution)/shard_map/ppermute | solution.py:119
  77.7 23.3 %collective-permute-start.20 = (bf16[144,2048]{1,0:T(8,128)(2,1)S(1)}, bf16[144,2048]{1,0:T(8,128)(2,1)}, u32[]{:S(2)}, u32[]{:S(2)}) collective-permute-start(bf16[144,2048]{1,0:T(8,128)(2,1)S(1)} %broadcast_select_fusion.refs_7_.refs_0_), channel_id=1, source_target_pairs={{8,0},{9,1},{10,2},{11,3},{12,4},{13,5},{14,6},{15,7},{16,8},{17,9... | collective-permute-start | bytes 1769480 | tf_op jit(solution)/shard_map/ppermute | solution.py:119
  79.9 17.1 %collective-permute-start.5 = (bf16[96,2048]{1,0:T(8,128)(2,1)}, bf16[96,2048]{1,0:T(8,128)(2,1)S(1)}, u32[]{:S(2)}, u32[]{:S(2)}) collective-permute-start(bf16[96,2048]{1,0:T(8,128)(2,1)} %collective-permute-done.4.refs_2_), channel_id=1, source_target_pairs={{16,24},{17,25},{18,26},{19,27},{20,28},{21,29},{22,30},{23,31}} | collective-permute-start | bytes 1179656 | tf_op jit(solution)/shard_map/ppermute | solution.py:119
  80.6 18.2 %collective-permute-start.8 = (bf16[96,2048]{1,0:T(8,128)(2,1)S(1)}, bf16[96,2048]{1,0:T(8,128)(2,1)S(1)}, u32[]{:S(2)}, u32[]{:S(2)}) collective-permute-start(bf16[96,2048]{1,0:T(8,128)(2,1)S(1)} %collective-permute-done.7.refs_5_), channel_id=1, source_target_pairs={{8,0},{9,1},{10,2},{11,3},{12,4},{13,5},{14,6},{15,7}} | collective-permute-start | bytes 1179656 | tf_op jit(solution)/shard_map/ppermute | solution.py:119
  96.9 25.3 %collective-permute-start.11 = (bf16[256,2048]{1,0:T(8,128)(2,1)S(1)}, bf16[256,2048]{1,0:T(8,128)(2,1)}, u32[]{:S(2)}, u32[]{:S(2)}) collective-permute-start(bf16[256,2048]{1,0:T(8,128)(2,1)S(1)} %collective-permute-done.10.refs_9_.refs_6_.refs_5_), channel_id=1, source_target_pairs={{0,1},{1,0},{2,3},{3,2},{4,5},{5,4},{6,7},{7,6},{8,9},{9,8},{10,11... | collective-permute-start | bytes 3145736 | tf_op jit(solution)/shard_map/ppermute | solution.py:119
  97.7 24.5 %collective-permute-start.13 = (bf16[256,2048]{1,0:T(8,128)(2,1)}, bf16[256,2048]{1,0:T(8,128)(2,1)}, u32[]{:S(2)}, u32[]{:S(2)}) collective-permute-start(bf16[256,2048]{1,0:T(8,128)(2,1)} %collective-permute-done.12.refs_11_.refs_8_.refs_7_), channel_id=1, source_target_pairs={{0,1},{1,0},{2,3},{3,2},{4,5},{5,4},{6,7},{7,6},{8,9},{9,8},{10,11... | collective-permute-start | bytes 3145736 | tf_op jit(solution)/shard_map/ppermute | solution.py:119
  99.5 49.0 %collective-permute-start.9 = (bf16[512,2048]{1,0:T(8,128)(2,1)S(1)}, bf16[512,2048]{1,0:T(8,128)(2,1)}, u32[]{:S(2)}, u32[]{:S(2)}) collective-permute-start(bf16[512,2048]{1,0:T(8,128)(2,1)S(1)} %copy-done), channel_id=1, source_target_pairs={{0,1},{1,0},{2,3},{3,2},{4,5},{5,4},{6,7},{7,6},{8,9},{9,8},{10,11... | collective-permute-start | bytes 6291464 | tf_op jit(solution)/shard_map/ppermute | solution.py:119
  99.5 6.6 %collective-permute-start.25 = (bf16[144,2048]{1,0:T(8,128)(2,1)}, bf16[144,2048]{1,0:T(8,128)(2,1)}, u32[]{:S(2)}, u32[]{:S(2)}) collective-permute-start(bf16[144,2048]{1,0:T(8,128)(2,1)} %collective-permute-done.19.refs_8_.refs_0_.refs_1_), channel_id=1, source_target_pairs={{8,16},{9,17},{10,18},{11,19},{12,20},{13,21},{14,22},{15,23},{16,... | collective-permute-start | bytes 1769480 | tf_op jit(solution)/shard_map/ppermute | solution.py:119
  101.0 19.4 %collective-permute-start.27 = (bf16[144,2048]{1,0:T(8,128)(2,1)}, bf16[144,2048]{1,0:T(8,128)(2,1)}, u32[]{:S(2)}, u32[]{:S(2)}) collective-permute-start(bf16[144,2048]{1,0:T(8,128)(2,1)} %collective-permute-done.20.refs_9_.refs_2_), channel_id=1, source_target_pairs={{8,0},{9,1},{10,2},{11,3},{12,4},{13,5},{14,6},{15,7},{16,8},{17,9... | collective-permute-start | bytes 1769480 | tf_op jit(solution)/shard_map/ppermute | solution.py:119
  106.2 25.9 %collective-permute-start.21 = (bf16[256,2048]{1,0:T(8,128)(2,1)}, bf16[256,2048]{1,0:T(8,128)(2,1)}, u32[]{:S(2)}, u32[]{:S(2)}) collective-permute-start(bf16[256,2048]{1,0:T(8,128)(2,1)} %collective-permute-done.12.refs_11_.refs_8_.refs_7_), channel_id=1, source_target_pairs={{0,2},{1,3},{2,0},{3,1},{4,6},{5,7},{6,4},{7,5},{8,10},{9,11},{10,... | collective-permute-start | bytes 3145736 | tf_op jit(solution)/shard_map/ppermute | solution.py:119
  120.4 24.9 %collective-permute-start.23 = (bf16[256,2048]{1,0:T(8,128)(2,1)S(1)}, bf16[256,2048]{1,0:T(8,128)(2,1)}, u32[]{:S(2)}, u32[]{:S(2)}) collective-permute-start(bf16[256,2048]{1,0:T(8,128)(2,1)S(1)} %collective-permute-done.10.refs_9_.refs_6_.refs_5_), channel_id=1, source_target_pairs={{0,4},{1,5},{2,6},{3,7},{4,0},{5,1},{6,2},{7,3},{8,12},{9,13},{10,... | collective-permute-start | bytes 3145736 | tf_op jit(solution)/shard_map/ppermute | solution.py:119
  122.2 23.2 %collective-permute-start.15 = (bf16[256,2048]{1,0:T(8,128)(2,1)}, bf16[256,2048]{1,0:T(8,128)(2,1)}, u32[]{:S(2)}, u32[]{:S(2)}) collective-permute-start(bf16[256,2048]{1,0:T(8,128)(2,1)} %collective-permute-done.14.refs_13_.refs_10_.refs_9_), channel_id=1, source_target_pairs={{0,1},{1,0},{2,3},{3,2},{4,5},{5,4},{6,7},{7,6},{8,9},{9,8},{10,11... | collective-permute-start | bytes 3145736 | tf_op jit(solution)/shard_map/ppermute | solution.py:119
  122.3 24.7 %collective-permute-start.17 = (bf16[256,2048]{1,0:T(8,128)(2,1)}, bf16[256,2048]{1,0:T(8,128)(2,1)}, u32[]{:S(2)}, u32[]{:S(2)}) collective-permute-start(bf16[256,2048]{1,0:T(8,128)(2,1)} %copy-done.1), channel_id=1, source_target_pairs={{0,1},{1,0},{2,3},{3,2},{4,5},{5,4},{6,7},{7,6},{8,9},{9,8},{10,11... | collective-permute-start | bytes 3145736 | tf_op jit(solution)/shard_map/ppermute | solution.py:119
  132.1 50.2 %collective-permute-start.22 = (bf16[256,2048]{1,0:T(8,128)(2,1)}, bf16[256,2048]{1,0:T(8,128)(2,1)S(1)}, u32[]{:S(2)}, u32[]{:S(2)}) collective-permute-start(bf16[256,2048]{1,0:T(8,128)(2,1)} %collective-permute-done.21.refs_10_.refs_14_), channel_id=1, source_target_pairs={{0,1},{1,0},{2,3},{3,2},{4,5},{5,4},{6,7},{7,6},{8,9},{9,8},{10,11... | collective-permute-start | bytes 3145736 | tf_op jit(solution)/shard_map/ppermute | solution.py:119
  145.3 37.0 %collective-permute-start.24 = (bf16[256,2048]{1,0:T(8,128)(2,1)}, bf16[256,2048]{1,0:T(8,128)(2,1)S(1)}, u32[]{:S(2)}, u32[]{:S(2)}) collective-permute-start(bf16[256,2048]{1,0:T(8,128)(2,1)} %collective-permute-done.23.refs_12_.refs_16_), channel_id=1, source_target_pairs={{0,1},{1,0},{2,3},{3,2},{4,5},{5,4},{6,7},{7,6},{8,9},{9,8},{10,11... | collective-permute-start | bytes 3145736 | tf_op jit(solution)/shard_map/ppermute | solution.py:119
  145.4 79.1 %collective-permute-start.33 = (s32[4,16]{1,0:T(4,128)S(1)}, s32[4,16]{1,0:T(4,128)S(1)}, u32[]{:S(2)}, u32[]{:S(2)}) collective-permute-start(s32[4,16]{1,0:T(4,128)S(1)} %get-tuple-element.30), channel_id=1, source_target_pairs={{0,4},{1,5},{2,6},{3,7},{4,0},{5,1},{6,2},{7,3},{8,12},{9,13},{10,... | collective-permute-start | bytes 776 | tf_op jit(solution)/shard_map/ppermute | solution.py:119
  147.0 43.0 %collective-permute-start.26 = (bf16[144,2048]{1,0:T(8,128)(2,1)}, bf16[144,2048]{1,0:T(8,128)(2,1)}, u32[]{:S(2)}, u32[]{:S(2)}) collective-permute-start(bf16[144,2048]{1,0:T(8,128)(2,1)} %collective-permute-done.25.refs_0_.refs_1_), channel_id=1, source_target_pairs={{16,24},{17,25},{18,26},{19,27},{20,28},{21,29},{22,30},{23,31}} | collective-permute-start | bytes 1769480 | tf_op jit(solution)/shard_map/ppermute | solution.py:119
  148.5 41.5 %collective-permute-start.28 = (bf16[144,2048]{1,0:T(8,128)(2,1)}, bf16[144,2048]{1,0:T(8,128)(2,1)}, u32[]{:S(2)}, u32[]{:S(2)}) collective-permute-start(bf16[144,2048]{1,0:T(8,128)(2,1)} %collective-permute-done.27.refs_2_.refs_3_), channel_id=1, source_target_pairs={{8,0},{9,1},{10,2},{11,3},{12,4},{13,5},{14,6},{15,7}} | collective-permute-start | bytes 1769480 | tf_op jit(solution)/shard_map/ppermute | solution.py:119
  218.6 6.1 %collective-permute-start.29 = (f32[4,4,240]{2,1,0:T(4,128)S(1)}, f32[4,4,240]{2,1,0:T(4,128)S(1)}, u32[]{:S(2)}, u32[]{:S(2)}) collective-permute-start(f32[4,4,240]{2,1,0:T(4,128)S(1)} %pad_maximum_fusion), channel_id=1, source_target_pairs={{0,8},{1,9},{2,10},{3,11},{4,12},{5,13},{6,14},{7,15},{8,16},{9,17... | collective-permute-start | bytes 46088 | tf_op jit(solution)/shard_map/ppermute | solution.py:119
  222.0 4.6 %collective-permute-start.30 = (f32[4,4,240]{2,1,0:T(4,128)S(1)}, f32[4,4,240]{2,1,0:T(4,128)S(1)}, u32[]{:S(2)}, u32[]{:S(2)}) collective-permute-start(f32[4,4,240]{2,1,0:T(4,128)S(1)} %pad_maximum_fusion), channel_id=1, source_target_pairs={{0,16},{1,17},{2,18},{3,19},{4,20},{5,21},{6,22},{7,23},{8,24},{9,... | collective-permute-start | bytes 46088 | tf_op jit(solution)/shard_map/ppermute | solution.py:119
  222.0 4.6 %collective-permute-start.31 = (f32[4,4,240]{2,1,0:T(4,128)S(1)}, f32[4,4,240]{2,1,0:T(4,128)S(1)}, u32[]{:S(2)}, u32[]{:S(2)}) collective-permute-start(f32[4,4,240]{2,1,0:T(4,128)S(1)} %pad_maximum_fusion), channel_id=1, source_target_pairs={{0,24},{1,25},{2,26},{3,27},{4,28},{5,29},{6,30},{7,31},{8,0},{9,1... | collective-permute-start | bytes 46088 | tf_op jit(solution)/shard_map/ppermute | solution.py:119
  (29 other events, 254.4 us)

commit v2 on v0

--- a/solution.py
+++ b/solution.py
@@ -1,9 +1,16 @@
+import functools
+
 import jax
 import jax.numpy as jnp
 from jax import lax
+from jax.experimental import pallas as pl
+from jax.experimental.pallas import tpu as pltpu
 from jax.sharding import PartitionSpec as P
 
 EPS = 1e-06
+LOW = -1e30
+BOTH = ("tok", "vocab")
+TOK, VOCAB, NZ, NY = 8, 4, 4, 2
 
 
 def combined_all(value, axis, join):
@@ -17,7 +24,7 @@
 def normalize(states, gain):
     values = states.astype(jnp.float32)
     scale_inv = lax.rsqrt(jnp.mean(values * values, axis=-1, keepdims=True) + EPS)
-    return (values * scale_inv * gain[None, :]).astype(jnp.bfloat16)
+    return (values * scale_inv * gain).astype(jnp.bfloat16)
 
 
 def combine(left_part, right_part):
@@ -33,7 +40,7 @@
 
 
 def score(states, wanted, gain, head):
-    normed = normalize(states, gain)
+    normed = normalize(states, gain[None, :])
     logits = jnp.einsum(
         "nd,vd->nv",
         normed,
@@ -59,7 +66,7 @@
     return (picked - log_total, log_total - moment / exp_total)
 
 
-def on_device(hidden, gain, head, targets, lengths, group_map):
+def on_any_mesh(hidden, gain, head, targets, lengths, group_map):
     capacity = hidden.shape[0]
     own_load = jnp.sum(lengths)
     slot_index = jnp.arange(capacity, dtype=jnp.int32)
@@ -94,9 +101,496 @@
     )
 
 
+def device_pairs(target):
+    pairs = []
+    for z in range(NZ):
+        for y in range(NY):
+            for x in range(2):
+                for c in range(2):
+                    to = target(z, y, x, c)
+                    if to is not None:
+                        pairs.append(
+                            ((z * NY + y) * VOCAB + x * 2 + c, (to[0] * NY + to[1]) * VOCAB + to[2] * 2 + to[3])
+                        )
+    return pairs
+
+
+def send(value, target):
+    return lax.ppermute(value, BOTH, device_pairs(target))
+
+
+def to_x(value):
+    return send(value, lambda z, y, x, c: (z, y, 1 - x, c))
+
+
+def to_y(value):
+    return send(value, lambda z, y, x, c: (z, 1 - y, x, c))
+
+
+def to_core(value):
+    return send(value, lambda z, y, x, c: (z, y, x, 1 - c))
+
+
+def across(value, step):
+    return send(value, lambda z, y, x, c: (z ^ step, y, x, c))
+
+
+SHARE = 384
+EVEN = 240
+SURE = 96
+REST = EVEN - SURE
+TILE = 256
+NOTES = TILE - EVEN
+PIECE = 256
+GROUP = 2 * PIECE
+
+
+def prep_kernel(which, h0, h1, h2, h3, gain_ref, tgt_ref, sure_ref, own_ref, trade_ref):
+    gain = gain_ref[...]
+    slots_count = tgt_ref.shape[1]
+    row = lax.broadcasted_iota(jnp.int32, (SURE, SURE), 0)
+    col = lax.broadcasted_iota(jnp.int32, (SURE, SURE), 1)
+    mirror = (row + col == SURE - 1).astype(jnp.bfloat16)
+
+    def flip(block):
+        return jnp.dot(mirror, block, preferred_element_type=jnp.float32).astype(jnp.bfloat16)
+
+    sure_ref[...] = normalize(h0[...], gain)
+    own_ref[0:SURE, :] = normalize(h1[...], gain)
+    third = normalize(h2[...], gain)
+    own_ref[SURE:REST, :] = third[0 : REST - SURE, :]
+    trade_ref[0:SURE, :] = flip(normalize(h3[...], gain))
+    trade_ref[SURE:REST, :] = flip(third)[0 : REST - SURE, :]
+
+    wanted = tgt_ref[...]
+    level = lax.broadcasted_iota(jnp.int32, (NOTES, slots_count), 0)
+    digits = jnp.where(level == 0, wanted & 127, jnp.where(level == 1, wanted >> 7, 0))
+    digits = digits.astype(jnp.float32).astype(jnp.bfloat16)
+    source = lax.broadcasted_iota(jnp.int32, (slots_count, TILE), 0)
+    lane = lax.broadcasted_iota(jnp.int32, (1, TILE), 1)
+
+    def notes(local, keep):
+        block = (
+            (local >= SURE).astype(jnp.int32)
+            + (local >= 2 * SURE).astype(jnp.int32)
+            + (local >= 3 * SURE).astype(jnp.int32)
+        )
+        at = local + block * ((VOCAB - 1) * SURE) + which[0] * SURE
+        at = jnp.where(keep, at, -1)
+        pick = jnp.where(source == at, 1.0, 0.0).astype(jnp.bfloat16)
+        return jnp.dot(digits, pick, preferred_element_type=jnp.float32).astype(jnp.bfloat16)
+
+    own_ref[REST : REST + NOTES, :] = jnp.zeros((NOTES, own_ref.shape[1]), jnp.bfloat16)
+    own_ref[REST : REST + NOTES, 0:TILE] = notes(lane, lane < EVEN)
+    trade_ref[REST : REST + NOTES, :] = jnp.zeros((NOTES, own_ref.shape[1]), jnp.bfloat16)
+    trade_ref[REST : REST + NOTES, 0:TILE] = notes(
+        2 * EVEN - 1 - lane, (lane >= SURE) & (lane < EVEN)
+    )
+
+
+def prepare(hidden, gain, targets, quarter):
+    width = hidden.shape[1]
+
+    def block(j):
+        return pl.BlockSpec((SURE, width), lambda i, which, j=j: (VOCAB * j + which[0], 0))
+
+    def whole(*shape):
+        return pl.BlockSpec(shape, lambda i, which: (0, 0))
+
+    return pl.pallas_call(
+        prep_kernel,
+        grid_spec=pltpu.PrefetchScalarGridSpec(
+            num_scalar_prefetch=1,
+            grid=(1,),
+            in_specs=[block(j) for j in range(4)] + [whole(1, width), whole(1, targets.shape[0])],
+            out_specs=[whole(n, width) for n in (SURE, REST + NOTES, REST + NOTES)],
+        ),
+        out_shape=[
+            jax.ShapeDtypeStruct((n, width), jnp.bfloat16) for n in (SURE, REST + NOTES, REST + NOTES)
+        ],
+        cost_estimate=pl.CostEstimate(flops=4 * 10**8, bytes_accessed=3 * 10**6, transcendentals=SHARE),
+        name="prep",
+    )(quarter.reshape(1), hidden, hidden, hidden, hidden, gain[None, :], targets[None, :])
+
+
+def merge_kernel(live_ref, own_ref, traded_ref, sizes_ref, out_ref):
+    live = live_ref[0]
+    for low in range(0, REST, 48):
+        slot = lax.broadcasted_iota(jnp.int32, (48, own_ref.shape[1]), 0) + (SURE + low)
+        out_ref[low : low + 48, :] = jnp.where(
+            slot < live,
+            own_ref[low : low + 48, :].astype(jnp.float32),
+            traded_ref[low : low + 48, :].astype(jnp.float32),
+        ).astype(jnp.bfloat16)
+    lane = lax.broadcasted_iota(jnp.int32, (NOTES, TILE), 1)
+    out_ref[REST : REST + NOTES, :] = jnp.zeros((NOTES, own_ref.shape[1]), jnp.bfloat16)
+    out_ref[REST : REST + NOTES, 0:TILE] = (
+        jnp.where(
+            lane < live,
+            own_ref[REST : REST + NOTES, 0:TILE].astype(jnp.float32),
+            traded_ref[REST : REST + NOTES, 0:TILE].astype(jnp.float32),
+        )
+        + sizes_ref[...]
+    ).astype(jnp.bfloat16)
+
+
+def merge(live, own, traded, sizes):
+    def whole(array):
+        return pl.BlockSpec(array.shape, lambda i, s: (0, 0))
+
+    return pl.pallas_call(
+        merge_kernel,
+        grid_spec=pltpu.PrefetchScalarGridSpec(
+            num_scalar_prefetch=1,
+            grid=(1,),
+            in_specs=[whole(own), whole(traded), whole(sizes)],
+            out_specs=whole(own),
+        ),
+        out_shape=jax.ShapeDtypeStruct(own.shape, own.dtype),
+        cost_estimate=pl.CostEstimate(flops=10**6, bytes_accessed=3 * 10**6, transcendentals=0),
+        name="merge",
+    )(live.reshape(1), own, traded, sizes)
+
+
+def stats_kernel(units, n_sets, n_known, final, head_plan, scalars, *refs):
+    known_ref = refs[0] if n_known else None
+    refs = refs[1:] if n_known else refs
+    tok_refs = refs[: 2 * n_sets]
+    n_head_refs = 1 + max(index for index, _ in head_plan)
+    head_refs = refs[2 * n_sets : 2 * n_sets + n_head_refs]
+    (out_ref, tok_buf, head_buf, logit_buf, state, wanted_buf, tok_sem, head_sem) = refs[
+        2 * n_sets + n_head_refs :
+    ]
+    n_groups = len(head_plan) // 2
+    n_units = len(units)
+    at_set, at_group, at_base = 2, 2 + n_units + 1, 2 + 2 * (n_units + 1)
+    z, offset = scalars[0], scalars[1]
+    lanes = (8, TILE)
+
+    def fetch(g):
+        for piece in (2 * g, 2 * g + 1):
+            index, start = head_plan[piece]
+            pltpu.make_async_copy(
+                head_refs[index].at[pl.ds(start, PIECE)],
+                head_buf.at[pl.ds(piece * PIECE, PIECE)],
+                head_sem.at[piece],
+            ).start()
+
+    def tok_copy(half):
+        return pltpu.make_async_copy(
+            tok_refs[half],
+            tok_buf.at[half // 2, pl.ds(SURE * (half % 2), tok_refs[half].shape[0])],
+            tok_sem.at[half],
+        )
+
+    for half in range(2 * n_sets):
+        tok_copy(half).start()
+    for g in range(min(2, n_groups)):
+        fetch(g)
+    logit_buf[...] = jnp.full(logit_buf.shape, LOW, jnp.float32)
+    for k in range(n_sets):
+        state[k, 0] = jnp.full(lanes, LOW, jnp.float32)
+        for row in range(1, 4):
+            state[k, row] = jnp.zeros(lanes, jnp.float32)
+    if not final:
+        for k in range(n_known):
+            for row in range(4):
+                state[k, row, 0:1, :] = known_ref[k, row : row + 1, :]
+    notes = []
+    for k in range(n_sets):
+        tok_copy(2 * k).wait()
+        tok_copy(2 * k + 1).wait()
+        digits = tok_buf[k, EVEN:TILE, 0:TILE].astype(jnp.float32)
+        wanted_buf[k] = (digits[0:1, :] + 128.0 * digits[1:2, :]).astype(jnp.int32) - offset
+        notes.append(digits[2:3, :] + 128.0 * digits[3:4, :])
+    chunk = 64
+    rows = lax.broadcasted_iota(jnp.int32, (chunk // 8,) + lanes, 0) * 8 + lax.broadcasted_iota(
+        jnp.int32, (chunk // 8,) + lanes, 1
+    )
+
+    def part(row):
+        return logit_buf[row : row + chunk, :].reshape((chunk // 8,) + lanes)
+
+    def reduce(entry):
+        k, g = scalars[at_set + entry], scalars[at_group + entry]
+        top_before = state[k, 0]
+        top = top_before
+        for row in range(0, GROUP, chunk):
+            top = jnp.maximum(top, jnp.max(part(row), axis=0))
+        shift = top_before - top
+        scale = jnp.exp(shift)
+        total_before = state[k, 1]
+        total = total_before * scale
+        moment = (state[k, 2] + shift * total_before) * scale
+        picked = state[k, 3]
+        for half in range(2):
+            wanted = wanted_buf[k] - scalars[at_base + 2 * g + half]
+            for row in range(0, PIECE, chunk):
+                logits = part(half * PIECE + row)
+                under = logits - top[None]
+                weight = jnp.exp(under)
+                total += jnp.sum(weight, axis=0)
+                moment += jnp.sum(weight * under, axis=0)
+                picked += jnp.sum(jnp.where(rows == (wanted - row)[None], logits, 0.0), axis=0)
+        state[k, 0] = top
+        state[k, 1] = total
+        state[k, 2] = moment
+        state[k, 3] = picked
+
+    def body(u, carry):
+        for ahead in range(2, n_groups):
+
+            @pl.when(u + 2 == ahead)
+            def _():
+                fetch(ahead)
+
+        @pl.when(u < n_groups)
+        def _():
+            for half in range(2):
+                pltpu.make_async_copy(
+                    head_refs[0].at[pl.ds(0, PIECE)],
+                    head_buf.at[pl.ds(u * GROUP + half * PIECE, PIECE)],
+                    head_sem.at[2 * u + half],
+                ).wait()
+
+        reduce(u)
+        k, g = scalars[at_set + u + 1], scalars[at_group + u + 1]
+        logit_buf[...] = lax.dot_general(
+            head_buf[pl.ds(pl.multiple_of(g * GROUP, GROUP), GROUP), :],
+            tok_buf[k],
+            (((1,), (1,)), ((), ())),
+            preferred_element_type=jnp.float32,
+        )
+        return carry
+
+    lax.fori_loop(0, n_units, body, 0)
+    reduce(n_units)
+    for k in range(n_sets):
+        top8 = state[k, 0]
+        top = jnp.max(top8, axis=0, keepdims=True)
+        shift = top8 - top
+        scale = jnp.exp(shift)
+        to = out_ref.at[z ^ (NZ - 1)] if final else out_ref.at[k]
+        to[0:1, :] = top
+        to[1:2, :] = jnp.sum(state[k, 1] * scale, axis=0, keepdims=True)
+        to[2:3, :] = jnp.sum((state[k, 2] + shift * state[k, 1]) * scale, axis=0, keepdims=True)
+        to[3:4, :] = jnp.sum(state[k, 3], axis=0, keepdims=True)
+        to[4:5, :] = notes[k]
+        to[5:8, :] = jnp.zeros((3, TILE), jnp.float32)
+    if final:
+        for k in range(n_known):
+            out_ref[z ^ k] = known_ref[k]
+
+
+def statistics(name, z, offset, sets, heads, plan, known=None, final=False):
+    arrays, head_plan = [], []
+    for array, start, _ in heads:
+        for index, seen in enumerate(arrays):
+            if seen is array:
+                break
+        else:
+            index = len(arrays)
+            arrays.append(array)
+        head_plan.append((index, start))
+    n_groups = len(heads) // 2
+    units = [(k, g) for k, first, last in plan for g in range(first, last)]
+    fixed = [units[0][0]] + [k for k, _ in units] + [n_groups] + [g for _, g in units]
+    scalars = jnp.concatenate(
+        [
+            jnp.stack([z, offset]),
+            jnp.array(fixed, jnp.int32),
+            jnp.stack([base for _, _, base in heads]),
+            jnp.array([1 << 30, 1 << 30], jnp.int32),
+        ]
+    ).astype(jnp.int32)
+    width = arrays[0].shape[1]
+    vocab = len(heads) * PIECE
+    before = [] if known is None else [known]
+    n_known = 0 if known is None else known.shape[0]
+    n_out = NZ if final else len(sets)
+    pairs = len(units) * GROUP * TILE
+    return pl.pallas_call(
+        functools.partial(stats_kernel, units, len(sets), n_known, final, head_plan),
+        grid_spec=pltpu.PrefetchScalarGridSpec(
+            num_scalar_prefetch=1,
+            grid=(1,),
+            in_specs=[pl.BlockSpec(array.shape, lambda i, s: (0, 0, 0)) for array in before]
+            + [pl.BlockSpec(memory_space=pl.ANY)] * (2 * len(sets) + len(arrays)),
+            out_specs=pl.BlockSpec((n_out, 8, TILE), lambda i, s: (0, 0, 0)),
+            scratch_shapes=[
+                pltpu.VMEM((len(sets), TILE, width), jnp.bfloat16),
+                pltpu.VMEM((vocab, width), jnp.bfloat16),
+                pltpu.VMEM((GROUP, TILE), jnp.float32),
+                pltpu.VMEM((len(sets), 4, 8, TILE), jnp.float32),
+                pltpu.VMEM((len(sets), 1, TILE), jnp.int32),
+                pltpu.SemaphoreType.DMA((2 * len(sets),)),
+                pltpu.SemaphoreType.DMA((len(heads),)),
+            ],
+        ),
+        out_shape=jax.ShapeDtypeStruct((n_out, 8, TILE), jnp.float32),
+        compiler_params=pltpu.CompilerParams(vmem_limit_bytes=58 * 1024 * 1024),
+        cost_estimate=pl.CostEstimate(
+            flops=2 * pairs * width,
+            bytes_accessed=2 * (len(sets) * TILE + vocab) * width,
+            transcendentals=pairs,
+        ),
+        name=name,
+    )(scalars, *before, *[half for pair in sets for half in pair], *arrays)
+
+
+def after(values, *deps):
+    return lax.optimization_barrier((values, deps))[0]
+
+
+def join(parts):
+    top = functools.reduce(jnp.maximum, [part[0] for part in parts])
+    total = moment = picked = 0.0
+    for part in parts:
+        shift = part[0] - top
+        scale = jnp.exp(shift)
+        total += part[1] * scale
+        moment += (part[2] + shift * part[1]) * scale
+        picked += part[3]
+    return top, total, moment, picked
+
+
+def on_device(hidden, gain, head, targets, lengths, group_map):
+    tok = lax.axis_index("tok")
+    vocab = lax.axis_index("vocab")
+    z, y = tok // NY, tok % NY
+    x, core = vocab // 2, vocab % 2
+    upper = z >= NZ // 2
+    quarter = jnp.where(upper, VOCAB - 1 - vocab, vocab)
+
+    zs = jnp.arange(NZ)
+
+    sure, rest_own, trade = prepare(hidden, gain, targets, quarter)
+    traded = across(trade, 2)
+    sizes_own = after(jnp.concatenate([lengths, group_map[:, 0]]), sure)
+    load = jnp.sum(sizes_own[:8])
+    block_start = (jnp.arange(4) * VOCAB + quarter) * SURE
+    live = jnp.sum(jnp.clip(load - block_start, 0, SURE))
+    level = jnp.arange(NOTES)[:, None]
+    sizes_own = jnp.pad(sizes_own, (0, TILE - 16))[None, :]
+    sizes_own = jnp.where(level == 2, sizes_own & 127, jnp.where(level == 3, sizes_own >> 7, 0))
+
+    rest = merge(live, rest_own, traded, sizes_own.astype(jnp.float32))
+    sure_1, sure_2 = across(sure, 1), across(after(sure, traded), 2)
+    rest_1, rest_2 = across(rest, 1), across(rest, 2)
+    sure_3 = across(sure_2, 1)
+
+    low_half, high_half = head[:PIECE], head[PIECE:]
+    xa, ya = to_x(low_half), to_y(high_half)
+    high_later, low_later = after((high_half, low_half), xa, ya)
+    xb, yb = to_x(high_later), to_y(low_later)
+
+    def base(at_y, at_x, at_core, half):
+        return ((at_y * 2 + at_x) * 2 + at_core) * GROUP + half * PIECE
+
+    def both_cores(piece, at_y, at_x, half):
+        return [
+            (piece, 0, base(at_y, at_x, core, half)),
+            (to_core(piece), 0, base(at_y, at_x, 1 - core, half)),
+        ]
+
+    head_core = to_core(head)
+    heads_own = [
+        (array, half * PIECE, base(y, x, at_core, half))
+        for array, at_core in ((head, core), (head_core, 1 - core))
+        for half in range(2)
+    ]
+    xa_later, ya_later = after((xa, ya), traded)
+    heads = heads_own + both_cores(xa_later, y, 1 - x, 0) + both_cores(ya_later, 1 - y, x, 1)
+    offset = z * (TOK * VOCAB // NZ * head.shape[0])
+    run = functools.partial(statistics, z=z, offset=offset)
+
+    x2, y2 = to_x(after(ya, xb, yb)), to_y(after(xa, xb, yb))
+    heads = heads + both_cores(xb, y, 1 - x, 1) + both_cores(yb, 1 - y, x, 0)
+    early = run(
+        "first",
+        sets=[(sure, rest), (sure_1, rest_1)],
+        heads=heads,
+        plan=[(0, 0, 6), (1, 0, 6)],
+    )
+    rest_2, sure_3, x2, y2 = after((rest_2, sure_3, x2, y2), early)
+    rest_3 = across(rest_2, 1)
+    heads = heads + both_cores(x2, 1 - y, 1 - x, 1) + both_cores(y2, 1 - y, 1 - x, 0)
+    early = run(
+        "second",
+        sets=[(sure, rest), (sure_1, rest_1), (sure_2, rest_2)],
+        heads=heads,
+        plan=[(2, 0, 8), (0, 6, 8), (1, 6, 8)],
+        known=early,
+    )
+    rest_3 = after(rest_3, early)
+    own_stats = run(
+        "third", sets=[(sure_3, rest_3)], heads=heads, plan=[(0, 0, 8)], known=early, final=True
+    )
+
+    parts = [own_stats] + [across(own_stats, step) for step in (1, 2, 3)]
+    top, total, moment, picked = join([jnp.moveaxis(part[:, :4, :EVEN], 1, 0) for part in parts])
+    spread = jnp.log(total)
+    logprob = picked - top - spread
+    entropy = spread - moment / total
+    partner = jnp.array([2, 3, 0, 1])
+    sizes = own_stats[:, 4, :16].astype(jnp.int32)
+    own_lengths = sizes[:, :8]
+    loads = jnp.sum(own_lengths, axis=1)
+    quarters = jnp.where(zs >= NZ // 2, VOCAB - 1 - vocab, vocab)
+    starts_of = (jnp.arange(4)[None, :] * VOCAB + quarters[:, None]) * SURE
+    lives = jnp.sum(jnp.clip(loads[:, None] - starts_of, 0, SURE), axis=1)
+    slots = jnp.arange(EVEN)
+    stays = slots[None, :] < lives[:, None]
+
+    local = jnp.where(stays, slots[None, :], 2 * EVEN - 1 - slots[None, :])
+    origin = jnp.where(stays, zs[:, None], partner[:, None])
+    origin_quarter = jnp.where(origin >= NZ // 2, VOCAB - 1 - vocab, vocab)
+    row = (local // SURE * VOCAB + origin_quarter) * SURE + local % SURE
+    place = origin * hidden.shape[0] + row
+    finish = jnp.cumsum(own_lengths, axis=1) + zs[:, None] * hidden.shape[0]
+    begin = finish - own_lengths
+    member = (place[:, :, None, None] >= begin) & (place[:, :, None, None] < finish)
+    sums_part = jnp.sum(jnp.where(member, logprob[:, :, None, None], 0.0), axis=(0, 1))
+
+    results = jnp.stack([logprob, entropy])
+    mine = lax.dynamic_index_in_dim(results, z, 1, False)
+    theirs = lax.dynamic_index_in_dim(results, z ^ 2, 1, False)
+    local_rows = jnp.concatenate([mine, jnp.flip(theirs[:, SURE:], 1)], 1)
+    local_rows = jnp.where(jnp.arange(SHARE)[None, :] < live, local_rows, 0.0)
+    gathered = lax.all_gather(
+        jnp.concatenate([local_rows.reshape(1, -1), sums_part.reshape(1, -1)], 1), "vocab"
+    ).reshape(VOCAB, -1)
+    sums_own = jnp.concatenate(
+        [
+            jnp.sum(gathered[:, 2 * SHARE :], axis=0).reshape(NZ, 8),
+            sizes.astype(jnp.float32),
+        ],
+        1,
+    )
+    sums_other = to_y(sums_own)
+    sums = jnp.where(
+        y == 0, jnp.stack([sums_own, sums_other], 1), jnp.stack([sums_other, sums_own], 1)
+    )
+    all_lengths, all_groups = sums[:, :, 8:16], sums[:, :, 16:].astype(jnp.int32)
+    sums = sums[:, :, :8]
+    parts = gathered[:, : 2 * SHARE].reshape(VOCAB, 2, SHARE)
+    parts = lax.dynamic_slice_in_dim(parts, vocab * SURE, SURE, 2)
+    parts = jnp.where(upper, jnp.flip(parts, 0), parts)
+    out = parts.transpose(1, 0, 2).reshape(2, SHARE)
+
+    means = (sums / all_lengths).reshape(-1)
+    onehot = (
+        all_groups.reshape(-1)[:, None] == jnp.arange(TOK, dtype=jnp.int32)[None, :]
+    ).astype(jnp.float32)
+    group_mean = jnp.sum(onehot * means[:, None], axis=0) / jnp.sum(onehot, axis=0)
+    centered = means - jnp.sum(onehot * group_mean[None, :], axis=1)
+    return out[0], out[1], lax.dynamic_slice_in_dim(centered, tok * 8 + vocab * 2, 2, 0)
+
+
 def solution(mesh):
+    fits = mesh.shape["tok"] == TOK and mesh.shape["vocab"] == VOCAB
     return jax.shard_map(
-        on_device,
+        on_device if fits else on_any_mesh,
         mesh=mesh,
         in_specs=(
             P("tok", None),

time: 338 us -> 160 us (0.47)
  waiting for transfers between devices: 226 us -> 61.1 us
  Pallas kernels: 0 us -> 46.7 us
  blocking collectives: 39.2 us -> 5.18 us
  matrix products: 34 us -> 0 us
  starting transfers between devices: 0.04 us -> 26.3 us
  other arithmetic: 22.5 us -> 6.92 us
  between operations: 14.2 us -> 0.9 us
  local copies, waits for them, and re-layouts: 1.66 us -> 12.7 us
    all_gather x1 -> x0, waiting for transfers between devices: 225 us -> none  [score(): lax.all_gather(head, 'tok', axis=0, tiled=True)]
    ppermute x0 -> x24, waiting for transfers between devices: none -> 61.1 us  [send(): return lax.ppermute(value, BOTH, device_pairs(target))]
    pallas_call x0 -> x5, Pallas kernels: none -> 46.7 us  [the longest x3 40 us: statistics(): pl.pallas_call(functools.partial(stats_kernel, units, len(sets), n_known,...]
    dot_general x1 -> x0, matrix products: 34 us -> none  [score(): jnp.einsum('nd,vd->nv', normed, lax.all_gather(head, 'tok', axis=0, tiled...]
    ppermute x0 -> x24, starting transfers between devices: none -> 26.3 us  [send(): return lax.ppermute(value, BOTH, device_pairs(target))]
    psum x1 -> x0, blocking collectives: 18.4 us -> none  [on_device(): lax.psum((jnp.sum(onehot * mean_logprob[:, None], axis=0), jnp.sum(onehot...]
    all_gather x4 -> x1, blocking collectives: 20.8 us -> 5.18 us  [on_device(): lax.all_gather(jnp.concatenate([local_rows.reshape(1, -1), sums_part.resh...]
    reduce_sum x4 -> x6, other arithmetic: 17.4 us -> 2.46 us  [the longest x1 1.36 us: on_device(): live = jnp.sum(jnp.clip(load - block_start, 0, SURE))]
  transfers between devices with their start and end apart: 1 -> 24, of which waited for: 1 -> 10; matrix products, arithmetic and copies ran while one was open for 2% -> 8% of each run, Pallas kernels for 0% -> 22%
where the time goes in v2:
time: 160 us
  waiting for transfers between devices  61.1 us (38%)
  Pallas kernels  46.7 us (29%)
  starting transfers between devices  26.3 us (16%)
  local copies, waits for them, and re-layouts  12.7 us (8%)
  other arithmetic  6.92 us (4%)
  blocking collectives  5.18 us (3%)
    ppermute x24, waiting for transfers between devices, send(): return lax.ppermute(value, BOTH, device_pairs(target))  61.1 us
    pallas_call x3, Pallas kernels, statistics(): pl.pallas_call(functools.partial(stats_kernel, units, len(sets), n_known,...  40 us
    ppermute x24, starting transfers between devices, send(): return lax.ppermute(value, BOTH, device_pairs(target))  26.3 us
    all_gather x1, blocking collectives, on_device(): lax.all_gather(jnp.concatenate([local_rows.reshape(1, -1), sums_part.resh...  5.18 us
    pallas_call x1, Pallas kernels, prepare(): pl.pallas_call(prep_kernel, grid_spec=pltpu.PrefetchScalarGridSpec(num_sc...  3.74 us
    concatenate x3, local copies, waits for them, and re-layouts, statistics(): jnp.concatenate([jnp.stack([z, offset]), jnp.array(fixed, jnp.int32), jnp...  3.36 us
  transfers between devices with their start and end apart: 24, of which 10 were waited for; matrix products, arithmetic and copies ran while one was open for 8% of the time, Pallas kernels for 22%

profile of v2, /device:TPU:0, one launch (start us, length us, event | category | flops | bytes accessed | tf_op | source)
XLA Modules:
  0.0 159.9 jit_solution(2447365662194308743)
XLA Ops:
  0.6 3.2 %fusion.34 = (bf16[256,2048]{1,0:T(8,128)(2,1)}, bf16[256,2048]{1,0:T(8,128)(2,1)}) fusion(bf16[512,2048]{1,0:T(8,128)(2,1)} %refs_3_.1), kind=kLoop, calls=%fused_computation.110 | loop fusion | bytes 4194304 | tf_op jit(solution)/shard_map/slice | solution.py:482
  3.8 2.9 %collective-permute-start.4 = (bf16[256,2048]{1,0:T(8,128)(2,1)}, bf16[256,2048]{1,0:T(8,128)(2,1)S(1)}, u32[]{:S(2)}, u32[]{:S(2)}) collective-permute-start(bf16[256,2048]{1,0:T(8,128)(2,1)} %get-tuple-element.26), channel_id=1, source_target_pairs={{0,2},{1,3},{2,0},{3,1},{4,6},{5,7},{6,4},{7,5},{8,10},{9,11},{10,... | collective-permute-start | bytes 3145736 | tf_op jit(solution)/shard_map/ppermute | solution.py:119
  6.8 1.5 collective-permute-start.5
  8.9 3.7 %prep.1 = (bf16[96,2048]{1,0:T(8,128)(2,1)}, bf16[160,2048]{1,0:T(8,128)(2,1)}, bf16[160,2048]{1,0:T(8,128)(2,1)}) custom-call(s32[1]{0:T(128)} %bitcast.1.which, bf16[1536,2048]{1,0:T(8,128)(2,1)} %h3.1, bf16[1536,2048]{1,0:T(8,128)(2,1)} %h3.1, bf16[1536,2048]{1,0:T(8,128)(2,1)} %h3.1, bf16[1536,2048]{1,0:T(8,128)(2,1)} %h3.1, f32[1,2048]{1,0:T(1,128)} %bitcast.139, ...), custom_call_target="tpu_custom_call" | custom-call | flops 400000000 | bytes 3000000 | tf_op jit(solution)/shard_map/prep/pallas_call | solution.py:200
  12.6 2.6 %collective-permute-start = (bf16[160,2048]{1,0:T(8,128)(2,1)}, bf16[160,2048]{1,0:T(8,128)(2,1)}, u32[]{:S(2)}, u32[]{:S(2)}) collective-permute-start(bf16[160,2048]{1,0:T(8,128)(2,1)} %get-tuple-element.22), channel_id=1, source_target_pairs={{0,16},{1,17},{2,18},{3,19},{4,20},{5,21},{6,22},{7,23},{8,24},{9,... | collective-permute-start | bytes 1966088 | tf_op jit(solution)/shard_map/ppermute | solution.py:119
  15.2 1.6 collective-permute-start.1
  17.5 12.6 %collective-permute-done.4.refs_6_.refs_9_.refs_5_ = bf16[256,2048]{1,0:T(8,128)(2,1)S(1)} collective-permute-done((bf16[256,2048]{1,0:T(8,128)(2,1)}, bf16[256,2048]{1,0:T(8,128)(2,1)S(1)}, u32[]{:S(2)}, u32[]{:S(2)}) %collective-permute-start.4) | collective-permute-done | bytes 1048608 | tf_op jit(solution)/shard_map/ppermute | solution.py:119
  30.1 1.6 collective-permute-done.5.refs_8_.refs_11_.refs_7_
  32.0 1.7 %collective-permute-start.10 = (bf16[256,2048]{1,0:T(8,128)(2,1)}, bf16[256,2048]{1,0:T(8,128)(2,1)}, u32[]{:S(2)}, u32[]{:S(2)}) collective-permute-start(bf16[256,2048]{1,0:T(8,128)(2,1)} %get-tuple-element.26), channel_id=1, source_target_pairs={{0,4},{1,5},{2,6},{3,7},{4,0},{5,1},{6,2},{7,3},{8,12},{9,13},{10,... | collective-permute-start | bytes 3145736 | tf_op jit(solution)/shard_map/ppermute | solution.py:119
  33.8 1.4 clamp_reduce_fusion.1
  35.1 8.7 %collective-permute-done.traded_ref = bf16[160,2048]{1,0:T(8,128)(2,1)} collective-permute-done((bf16[160,2048]{1,0:T(8,128)(2,1)}, bf16[160,2048]{1,0:T(8,128)(2,1)}, u32[]{:S(2)}, u32[]{:S(2)}) %collective-permute-start) | collective-permute-done | bytes 655392 | tf_op jit(solution)/shard_map/ppermute | solution.py:119
  44.5 3.0 %merge.1.refs_1_.refs_2_ = bf16[160,2048]{1,0:T(8,128)(2,1)} custom-call(s32[1]{0:T(128)} %bitcast.21.live_ref, bf16[160,2048]{1,0:T(8,128)(2,1)} %get-tuple-element.21.own_ref, bf16[160,2048]{1,0:T(8,128)(2,1)} %collective-permute-done.traded_ref, f32[16,256]{1,0:T(8,128)} %select_convert_fusion.sizes_ref), custom_call_target="tpu_custom_call" | custom-call | flops 1000000 | bytes 3000000 | tf_op jit(solution)/shard_map/merge/pallas_call | solution.py:241
  47.4 4.0 %collective-permute-start.2 = (bf16[160,2048]{1,0:T(8,128)(2,1)}, bf16[160,2048]{1,0:T(8,128)(2,1)S(1)}, u32[]{:S(2)}, u32[]{:S(2)}) collective-permute-start(bf16[160,2048]{1,0:T(8,128)(2,1)} %merge.1.refs_1_.refs_2_), channel_id=1, source_target_pairs={{0,8},{1,9},{2,10},{3,11},{4,12},{5,13},{6,14},{7,15},{8,0},{9,1},... | collective-permute-start | bytes 1966088 | tf_op jit(solution)/shard_map/ppermute | solution.py:119
  51.5 12.0 %collective-permute-done.12.refs_5_ = bf16[96,2048]{1,0:T(8,128)(2,1)} collective-permute-done((bf16[96,2048]{1,0:T(8,128)(2,1)}, bf16[96,2048]{1,0:T(8,128)(2,1)}, u32[]{:S(2)}, u32[]{:S(2)}) %collective-permute-start.12) | collective-permute-done | bytes 393248 | tf_op jit(solution)/shard_map/ppermute | solution.py:119
  63.5 9.2 %collective-permute-done.2.refs_3_.refs_4_ = bf16[160,2048]{1,0:T(8,128)(2,1)S(1)} collective-permute-done((bf16[160,2048]{1,0:T(8,128)(2,1)}, bf16[160,2048]{1,0:T(8,128)(2,1)S(1)}, u32[]{:S(2)}, u32[]{:S(2)}) %collective-permute-start.2) | collective-permute-done | bytes 655392 | tf_op jit(solution)/shard_map/ppermute | solution.py:119
  73.9 1.0 copy-done.2
  75.8 1.6 collective-permute-start.13
  78.0 2.4 %collective-permute-start.14 = (bf16[96,2048]{1,0:T(8,128)(2,1)}, bf16[96,2048]{1,0:T(8,128)(2,1)S(1)}, u32[]{:S(2)}, u32[]{:S(2)}) collective-permute-start(bf16[96,2048]{1,0:T(8,128)(2,1)} %collective-permute-done.12.refs_5_), channel_id=1, source_target_pairs={{0,8},{1,9},{2,10},{3,11},{4,12},{5,13},{6,14},{7,15},{8,0},{9,1},... | collective-permute-start | bytes 1179656 | tf_op jit(solution)/shard_map/ppermute | solution.py:119
  80.4 13.8 %first.1.refs_0_ = f32[2,8,256]{2,1,0:T(8,128)} custom-call(s32[42]{0:T(128)} %concatenate.24.scalars, bf16[96,2048]{1,0:T(8,128)(2,1)} %get-tuple-element.27.refs_0_.refs_1_, bf16[160,2048]{1,0:T(8,128)(2,1)} %merge.1.refs_1_.refs_2_, bf16[96,2048]{1,0:T(8,128)(2,1)} %copy-done.13, bf16[160,2048]{1,0:T(8,128)(2,1)} %copy-done.12, ...), custom_call_target="tpu_custom_call" | custom-call | flops 6442450944 | bytes 14680064 | tf_op jit(solution)/shard_map/first/pallas_call | solution.py:412
  94.3 13.5 %collective-permute-done.13.refs_6_ = bf16[160,2048]{1,0:T(8,128)(2,1)} collective-permute-done((bf16[160,2048]{1,0:T(8,128)(2,1)}, bf16[160,2048]{1,0:T(8,128)(2,1)}, u32[]{:S(2)}, u32[]{:S(2)}) %collective-permute-start.13) | collective-permute-done | bytes 655392 | tf_op jit(solution)/shard_map/ppermute | solution.py:119
  109.2 1.2 iota_compare_fusion.2
  110.4 1.3 concatenate.22.scalars
  111.7 1.3 concatenate.23.scalars
  113.1 0.9 copy-done.5
  114.0 15.0 %second.1.refs_0_ = f32[3,8,256]{2,1,0:T(8,128)} custom-call(s32[46]{0:T(128)} %concatenate.23.scalars, f32[2,8,256]{2,1,0:T(8,128)} %first.1.refs_0_, bf16[96,2048]{1,0:T(8,128)(2,1)} %get-tuple-element.27.refs_0_.refs_1_, bf16[160,2048]{1,0:T(8,128)(2,1)} %merge.1.refs_1_.refs_2_, bf16[96,2048]{1,0:T(8,128)(2,1)} %copy-done.13, ...), custom_call_target="tpu_custom_call" | custom-call | flops 6442450944 | bytes 19922944 | tf_op jit(solution)/shard_map/second/pallas_call | solution.py:412
  129.1 11.2 %third.1 = f32[4,8,256]{2,1,0:T(8,128)} custom-call(s32[38]{0:T(128)} %concatenate.22.scalars, f32[3,8,256]{2,1,0:T(8,128)} %second.1.refs_0_, bf16[96,2048]{1,0:T(8,128)(2,1)} %copy-done.6, bf16[160,2048]{1,0:T(8,128)(2,1)} %collective-permute-done.19.refs_2_, bf16[512,2048]{1,0:T(8,128)(2,1)} %refs_3_.1, ...), custom_call_target="tpu_custom_call" | custom-call | flops 4294967296 | bytes 17825792 | tf_op jit(solution)/shard_map/third/pallas_call | solution.py:412
  140.3 2.5 %collective-permute-start.22 = (f32[4,8,256]{2,1,0:T(8,128)}, f32[4,8,256]{2,1,0:T(8,128)S(1)}, u32[]{:S(2)}, u32[]{:S(2)}) collective-permute-start(f32[4,8,256]{2,1,0:T(8,128)} %third.1), channel_id=1, source_target_pairs={{0,24},{1,25},{2,26},{3,27},{4,28},{5,29},{6,30},{7,31},{8,16},{9,... | collective-permute-start | bytes 98312 | tf_op jit(solution)/shard_map/ppermute | solution.py:119
  143.6 1.1 collective-permute-start.21
  147.0 1.6 collective-permute-done.21
  149.7 5.2 %all-gather.1 = f32[4,1,800]{2,1,0:T(1,128)S(1)} all-gather(f32[1,1,800]{2,1,0:T(1,128)S(1)} %maximum_bitcast_fusion), channel_id=2, replica_groups=mesh['tok'=8,'vocab'=4] {'vocab'}, dimensions={0}, use_global_device_ids=true | all-gather | bytes 16000 | tf_op jit(solution)/shard_map/all_gather | solution.py:560
  155.2 1.0 collective-permute-start.23
  157.5 1.2 collective-permute-done.23
  (118 shorter events, 13.3 us)
Async XLA Ops:
  3.8 26.3 %collective-permute-start.4 = (bf16[256,2048]{1,0:T(8,128)(2,1)}, bf16[256,2048]{1,0:T(8,128)(2,1)S(1)}, u32[]{:S(2)}, u32[]{:S(2)}) collective-permute-start(bf16[256,2048]{1,0:T(8,128)(2,1)} %get-tuple-element.26), channel_id=1, source_target_pairs={{0,2},{1,3},{2,0},{3,1},{4,6},{5,7},{6,4},{7,5},{8,10},{9,11},{10,... | collective-permute-start | bytes 3145736 | tf_op jit(solution)/shard_map/ppermute | solution.py:119
  6.8 24.9 %collective-permute-start.5 = (bf16[256,2048]{1,0:T(8,128)(2,1)}, bf16[256,2048]{1,0:T(8,128)(2,1)}, u32[]{:S(2)}, u32[]{:S(2)}) collective-permute-start(bf16[256,2048]{1,0:T(8,128)(2,1)} %get-tuple-element.25), channel_id=1, source_target_pairs={{0,4},{1,5},{2,6},{3,7},{4,0},{5,1},{6,2},{7,3},{8,12},{9,13},{10,... | collective-permute-start | bytes 3145736 | tf_op jit(solution)/shard_map/ppermute | solution.py:119
  8.9 7.9 %copy-start.15 = (s32[8]{0:T(128)S(1)}, s32[8]{0:T(128)}, u32[]{:S(2)}) copy-start(s32[8]{0:T(128)} %param.17) | copy-start | bytes 100
  12.6 64.7 %copy-start.9 = (s32[26]{0:T(128)S(1)}, s32[26]{0:T(128)}, u32[]{:S(2)}) copy-start(s32[26]{0:T(128)} %constant.120.clone) | copy-start | bytes 316
  12.6 31.2 %collective-permute-start = (bf16[160,2048]{1,0:T(8,128)(2,1)}, bf16[160,2048]{1,0:T(8,128)(2,1)}, u32[]{:S(2)}, u32[]{:S(2)}) collective-permute-start(bf16[160,2048]{1,0:T(8,128)(2,1)} %get-tuple-element.22), channel_id=1, source_target_pairs={{0,16},{1,17},{2,18},{3,19},{4,20},{5,21},{6,22},{7,23},{8,24},{9,... | collective-permute-start | bytes 1966088 | tf_op jit(solution)/shard_map/ppermute | solution.py:119
  15.2 58.1 %collective-permute-start.3 = (bf16[512,2048]{1,0:T(8,128)(2,1)S(1)}, bf16[512,2048]{1,0:T(8,128)(2,1)}, u32[]{:S(2)}, u32[]{:S(2)}) collective-permute-start(bf16[512,2048]{1,0:T(8,128)(2,1)S(1)} %copy-done), channel_id=1, source_target_pairs={{0,1},{1,0},{2,3},{3,2},{4,5},{5,4},{6,7},{7,6},{8,9},{9,8},{10,11... | collective-permute-start | bytes 6291464 | tf_op jit(solution)/shard_map/ppermute | solution.py:119
  15.2 32.2 %collective-permute-start.1 = (bf16[96,2048]{1,0:T(8,128)(2,1)}, bf16[96,2048]{1,0:T(8,128)(2,1)S(1)}, u32[]{:S(2)}, u32[]{:S(2)}) collective-permute-start(bf16[96,2048]{1,0:T(8,128)(2,1)} %get-tuple-element.27.refs_0_.refs_1_), channel_id=1, source_target_pairs={{0,8},{1,9},{2,10},{3,11},{4,12},{5,13},{6,14},{7,15},{8,0},{9,1},... | collective-permute-start | bytes 1179656 | tf_op jit(solution)/shard_map/ppermute | solution.py:119
  30.1 50.3 %copy-start.1 = (bf16[256,2048]{1,0:T(8,128)(2,1)}, bf16[256,2048]{1,0:T(8,128)(2,1)S(1)}, u32[]{:S(2)}) copy-start(bf16[256,2048]{1,0:T(8,128)(2,1)S(1)} %collective-permute-done.4.refs_6_.refs_9_.refs_5_) | copy-start | bytes 3145732
  31.7 41.1 %collective-permute-start.8 = (bf16[256,2048]{1,0:T(8,128)(2,1)}, bf16[256,2048]{1,0:T(8,128)(2,1)}, u32[]{:S(2)}, u32[]{:S(2)}) collective-permute-start(bf16[256,2048]{1,0:T(8,128)(2,1)} %get-tuple-element.25), channel_id=1, source_target_pairs={{0,2},{1,3},{2,0},{3,1},{4,6},{5,7},{6,4},{7,5},{8,10},{9,11},{10,... | collective-permute-start | bytes 3145736 | tf_op jit(solution)/shard_map/ppermute | solution.py:119
  32.0 41.3 %collective-permute-start.10 = (bf16[256,2048]{1,0:T(8,128)(2,1)}, bf16[256,2048]{1,0:T(8,128)(2,1)}, u32[]{:S(2)}, u32[]{:S(2)}) collective-permute-start(bf16[256,2048]{1,0:T(8,128)(2,1)} %get-tuple-element.26), channel_id=1, source_target_pairs={{0,4},{1,5},{2,6},{3,7},{4,0},{5,1},{6,2},{7,3},{8,12},{9,13},{10,... | collective-permute-start | bytes 3145736 | tf_op jit(solution)/shard_map/ppermute | solution.py:119
  43.8 19.7 %collective-permute-start.12 = (bf16[96,2048]{1,0:T(8,128)(2,1)}, bf16[96,2048]{1,0:T(8,128)(2,1)}, u32[]{:S(2)}, u32[]{:S(2)}) collective-permute-start(bf16[96,2048]{1,0:T(8,128)(2,1)} %get-tuple-element.27.refs_0_.refs_1_), channel_id=1, source_target_pairs={{0,16},{1,17},{2,18},{3,19},{4,20},{5,21},{6,22},{7,23},{8,24},{9,... | collective-permute-start | bytes 1179656 | tf_op jit(solution)/shard_map/ppermute | solution.py:119
  47.4 29.9 %copy-start.13 = (bf16[96,2048]{1,0:T(8,128)(2,1)}, bf16[96,2048]{1,0:T(8,128)(2,1)S(1)}, u32[]{:S(2)}) copy-start(bf16[96,2048]{1,0:T(8,128)(2,1)S(1)} %collective-permute-done.1.refs_2_.refs_3_) | copy-start | bytes 1179652
  47.4 25.3 %collective-permute-start.2 = (bf16[160,2048]{1,0:T(8,128)(2,1)}, bf16[160,2048]{1,0:T(8,128)(2,1)S(1)}, u32[]{:S(2)}, u32[]{:S(2)}) collective-permute-start(bf16[160,2048]{1,0:T(8,128)(2,1)} %merge.1.refs_1_.refs_2_), channel_id=1, source_target_pairs={{0,8},{1,9},{2,10},{3,11},{4,12},{5,13},{6,14},{7,15},{8,0},{9,1},... | collective-permute-start | bytes 1966088 | tf_op jit(solution)/shard_map/ppermute | solution.py:119
  63.5 10.4 %collective-permute-start.6 = (bf16[256,2048]{1,0:T(8,128)(2,1)S(1)}, bf16[256,2048]{1,0:T(8,128)(2,1)S(1)}, u32[]{:S(2)}, u32[]{:S(2)}) collective-permute-start(bf16[256,2048]{1,0:T(8,128)(2,1)S(1)} %collective-permute-done.4.refs_6_.refs_9_.refs_5_), channel_id=1, source_target_pairs={{0,1},{1,0},{2,3},{3,2},{4,5},{5,4},{6,7},{7,6},{8,9},{9,8},{10,11... | collective-permute-start | bytes 3145736 | tf_op jit(solution)/shard_map/ppermute | solution.py:119
  72.7 3.0 %collective-permute-start.7 = (bf16[256,2048]{1,0:T(8,128)(2,1)}, bf16[256,2048]{1,0:T(8,128)(2,1)}, u32[]{:S(2)}, u32[]{:S(2)}) collective-permute-start(bf16[256,2048]{1,0:T(8,128)(2,1)} %collective-permute-done.5.refs_8_.refs_11_.refs_7_), channel_id=1, source_target_pairs={{0,1},{1,0},{2,3},{3,2},{4,5},{5,4},{6,7},{7,6},{8,9},{9,8},{10,11... | collective-permute-start | bytes 3145736 | tf_op jit(solution)/shard_map/ppermute | solution.py:119
  72.8 5.3 %collective-permute-start.9 = (bf16[256,2048]{1,0:T(8,128)(2,1)}, bf16[256,2048]{1,0:T(8,128)(2,1)}, u32[]{:S(2)}, u32[]{:S(2)}) collective-permute-start(bf16[256,2048]{1,0:T(8,128)(2,1)} %collective-permute-done.8.refs_10_.refs_13_.refs_9_), channel_id=1, source_target_pairs={{0,1},{1,0},{2,3},{3,2},{4,5},{5,4},{6,7},{7,6},{8,9},{9,8},{10,11... | collective-permute-start | bytes 3145736 | tf_op jit(solution)/shard_map/ppermute | solution.py:119
  73.3 7.1 %collective-permute-start.11 = (bf16[256,2048]{1,0:T(8,128)(2,1)}, bf16[256,2048]{1,0:T(8,128)(2,1)}, u32[]{:S(2)}, u32[]{:S(2)}) collective-permute-start(bf16[256,2048]{1,0:T(8,128)(2,1)} %collective-permute-done.10.refs_12_.refs_15_.refs_11_), channel_id=1, source_target_pairs={{0,1},{1,0},{2,3},{3,2},{4,5},{5,4},{6,7},{7,6},{8,9},{9,8},{10,11... | collective-permute-start | bytes 3145736 | tf_op jit(solution)/shard_map/ppermute | solution.py:119
  73.3 34.5 %collective-permute-start.15 = (bf16[256,2048]{1,0:T(8,128)(2,1)}, bf16[256,2048]{1,0:T(8,128)(2,1)S(1)}, u32[]{:S(2)}, u32[]{:S(2)}) collective-permute-start(bf16[256,2048]{1,0:T(8,128)(2,1)} %collective-permute-done.5.refs_8_.refs_11_.refs_7_), channel_id=1, source_target_pairs={{0,2},{1,3},{2,0},{3,1},{4,6},{5,7},{6,4},{7,5},{8,10},{9,11},{10,... | collective-permute-start | bytes 3145736 | tf_op jit(solution)/shard_map/ppermute | solution.py:119
  74.9 32.9 %collective-permute-start.16 = (bf16[256,2048]{1,0:T(8,128)(2,1)S(1)}, bf16[256,2048]{1,0:T(8,128)(2,1)S(1)}, u32[]{:S(2)}, u32[]{:S(2)}) collective-permute-start(bf16[256,2048]{1,0:T(8,128)(2,1)S(1)} %collective-permute-done.4.refs_6_.refs_9_.refs_5_), channel_id=1, source_target_pairs={{0,4},{1,5},{2,6},{3,7},{4,0},{5,1},{6,2},{7,3},{8,12},{9,13},{10,... | collective-permute-start | bytes 3145736 | tf_op jit(solution)/shard_map/ppermute | solution.py:119
  75.8 32.0 %collective-permute-start.13 = (bf16[160,2048]{1,0:T(8,128)(2,1)}, bf16[160,2048]{1,0:T(8,128)(2,1)}, u32[]{:S(2)}, u32[]{:S(2)}) collective-permute-start(bf16[160,2048]{1,0:T(8,128)(2,1)} %merge.1.refs_1_.refs_2_), channel_id=1, source_target_pairs={{0,16},{1,17},{2,18},{3,19},{4,20},{5,21},{6,22},{7,23},{8,24},{9,... | collective-permute-start | bytes 1966088 | tf_op jit(solution)/shard_map/ppermute | solution.py:119
  78.0 29.8 %collective-permute-start.14 = (bf16[96,2048]{1,0:T(8,128)(2,1)}, bf16[96,2048]{1,0:T(8,128)(2,1)S(1)}, u32[]{:S(2)}, u32[]{:S(2)}) collective-permute-start(bf16[96,2048]{1,0:T(8,128)(2,1)} %collective-permute-done.12.refs_5_), channel_id=1, source_target_pairs={{0,8},{1,9},{2,10},{3,11},{4,12},{5,13},{6,14},{7,15},{8,0},{9,1},... | collective-permute-start | bytes 1179656 | tf_op jit(solution)/shard_map/ppermute | solution.py:119
  107.8 21.3 %copy-start.6 = (bf16[96,2048]{1,0:T(8,128)(2,1)}, bf16[96,2048]{1,0:T(8,128)(2,1)S(1)}, u32[]{:S(2)}) copy-start(bf16[96,2048]{1,0:T(8,128)(2,1)S(1)} %collective-permute-done.14.refs_1_) | copy-start | bytes 1179652
  107.8 5.2 %collective-permute-start.17 = (bf16[256,2048]{1,0:T(8,128)(2,1)S(1)}, bf16[256,2048]{1,0:T(8,128)(2,1)S(1)}, u32[]{:S(2)}, u32[]{:S(2)}) collective-permute-start(bf16[256,2048]{1,0:T(8,128)(2,1)S(1)} %collective-permute-done.15.refs_17_.refs_13_), channel_id=1, source_target_pairs={{0,1},{1,0},{2,3},{3,2},{4,5},{5,4},{6,7},{7,6},{8,9},{9,8},{10,11... | collective-permute-start | bytes 3145736 | tf_op jit(solution)/shard_map/ppermute | solution.py:119
  107.9 5.2 %collective-permute-start.18 = (bf16[256,2048]{1,0:T(8,128)(2,1)S(1)}, bf16[256,2048]{1,0:T(8,128)(2,1)}, u32[]{:S(2)}, u32[]{:S(2)}) collective-permute-start(bf16[256,2048]{1,0:T(8,128)(2,1)S(1)} %collective-permute-done.16.refs_19_.refs_15_), channel_id=1, source_target_pairs={{0,1},{1,0},{2,3},{3,2},{4,5},{5,4},{6,7},{7,6},{8,9},{9,8},{10,11... | collective-permute-start | bytes 3145736 | tf_op jit(solution)/shard_map/ppermute | solution.py:119
  109.1 20.0 %collective-permute-start.19 = (bf16[160,2048]{1,0:T(8,128)(2,1)}, bf16[160,2048]{1,0:T(8,128)(2,1)}, u32[]{:S(2)}, u32[]{:S(2)}) collective-permute-start(bf16[160,2048]{1,0:T(8,128)(2,1)} %collective-permute-done.13.refs_6_), channel_id=1, source_target_pairs={{0,8},{1,9},{2,10},{3,11},{4,12},{5,13},{6,14},{7,15},{8,0},{9,1},... | collective-permute-start | bytes 1966088 | tf_op jit(solution)/shard_map/ppermute | solution.py:119
  129.1 17.4 %copy-start.10 = (s32[4]{0:T(128)S(1)}, s32[4]{0:T(128)}, u32[]{:S(2)}) copy-start(s32[4]{0:T(128)} %iota_multiply_fusion) | copy-start | bytes 52
  129.1 17.7 %copy-start.8 = (s32[4]{0:T(128)S(1)}, s32[4]{0:T(128)}, u32[]{:S(2)}) copy-start(s32[4]{0:T(128)} %constant.124.clone) | copy-start | bytes 52
  129.1 20.5 %copy-start.11 = (pred[384]{0:T(512)(128)(4,1)S(1)}, pred[384]{0:T(512)(128)(4,1)}, u32[]{:S(2)}) copy-start(pred[384]{0:T(512)(128)(4,1)} %iota_compare_fusion.2) | copy-start | bytes 1156
  140.3 6.7 %collective-permute-start.22 = (f32[4,8,256]{2,1,0:T(8,128)}, f32[4,8,256]{2,1,0:T(8,128)S(1)}, u32[]{:S(2)}, u32[]{:S(2)}) collective-permute-start(f32[4,8,256]{2,1,0:T(8,128)} %third.1), channel_id=1, source_target_pairs={{0,24},{1,25},{2,26},{3,27},{4,28},{5,29},{6,30},{7,31},{8,16},{9,... | collective-permute-start | bytes 98312 | tf_op jit(solution)/shard_map/ppermute | solution.py:119
  143.6 4.9 %collective-permute-start.21 = (f32[4,8,256]{2,0,1:T(4,128)S(1)}, f32[4,8,256]{2,0,1:T(4,128)S(1)}, u32[]{:S(2)}, u32[]{:S(2)}) collective-permute-start(f32[4,8,256]{2,0,1:T(4,128)S(1)} %copy.52), channel_id=1, source_target_pairs={{0,16},{1,17},{2,18},{3,19},{4,20},{5,21},{6,22},{7,23},{8,24},{9,... | collective-permute-start | bytes 98312 | tf_op jit(solution)/shard_map/ppermute | solution.py:119
  144.7 4.2 %collective-permute-start.20 = (f32[4,8,256]{2,0,1:T(4,128)S(1)}, f32[4,8,256]{2,0,1:T(4,128)S(1)}, u32[]{:S(2)}, u32[]{:S(2)}) collective-permute-start(f32[4,8,256]{2,0,1:T(4,128)S(1)} %copy.52), channel_id=1, source_target_pairs={{0,8},{1,9},{2,10},{3,11},{4,12},{5,13},{6,14},{7,15},{8,0},{9,1},... | collective-permute-start | bytes 98312 | tf_op jit(solution)/shard_map/ppermute | solution.py:119
  155.2 3.6 %collective-permute-start.23 = (f32[4,24]{1,0:T(4,128)S(1)}, f32[4,24]{1,0:T(4,128)S(1)}, u32[]{:S(2)}, u32[]{:S(2)}) collective-permute-start(f32[4,24]{1,0:T(4,128)S(1)} %pad_maximum_fusion), channel_id=1, source_target_pairs={{0,4},{1,5},{2,6},{3,7},{4,0},{5,1},{6,2},{7,3},{8,12},{9,13},{10,... | collective-permute-start | bytes 1160 | tf_op jit(solution)/shard_map/ppermute | solution.py:119
  (8 other events, 37.1 us)

commit v3 on v2

--- a/solution.py
+++ b/solution.py
@@ -428,7 +428,7 @@
             ],
         ),
         out_shape=jax.ShapeDtypeStruct((n_out, 8, TILE), jnp.float32),
-        compiler_params=pltpu.CompilerParams(vmem_limit_bytes=58 * 1024 * 1024),
+        compiler_params=pltpu.CompilerParams(vmem_limit_bytes=61 * 1024 * 1024),
         cost_estimate=pl.CostEstimate(
             flops=2 * pairs * width,
             bytes_accessed=2 * (len(sets) * TILE + vocab) * width,
@@ -479,7 +479,8 @@
     rest_1, rest_2 = across(rest, 1), across(rest, 2)
     sure_3 = across(sure_2, 1)
 
-    low_half, high_half = head[:PIECE], head[PIECE:]
+    head_later = after(head, sure)
+    low_half, high_half = head_later[:PIECE], head_later[PIECE:]
     xa, ya = to_x(low_half), to_y(high_half)
     high_later, low_later = after((high_half, low_half), xa, ya)
     xb, yb = to_x(high_later), to_y(low_later)

time: 160 us -> 158 us (0.988)
  local copies, waits for them, and re-layouts: 12.7 us -> 9.39 us
  waiting for transfers between devices: 61.1 us -> 63.7 us
    ppermute x24, waiting for transfers between devices: 61.1 us -> 63.7 us  [send(): return lax.ppermute(value, BOTH, device_pairs(target))]
    slice x1, local copies, waits for them, and re-layouts: 3.18 us -> 1.53 us  [on_device(): low_half, high_half = (head_later[:PIECE], head_later[PIECE:])]
  transfers between devices with their start and end apart: 24 -> 24, of which waited for: 10 -> 11; matrix products, arithmetic and copies ran while one was open for 8% -> 6% of each run, Pallas kernels for 22% -> 20%
where the time goes in v3:
time: 158 us
  waiting for transfers between devices  63.7 us (40%)
  Pallas kernels  46.7 us (30%)
  starting transfers between devices  25.9 us (16%)
  local copies, waits for them, and re-layouts  9.39 us (6%)
  other arithmetic  5.75 us (4%)
  blocking collectives  5.18 us (3%)
    ppermute x24, waiting for transfers between devices, send(): return lax.ppermute(value, BOTH, device_pairs(target))  63.7 us
    pallas_call x3, Pallas kernels, statistics(): pl.pallas_call(functools.partial(stats_kernel, units, len(sets), n_known,...  40 us
    ppermute x24, starting transfers between devices, send(): return lax.ppermute(value, BOTH, device_pairs(target))  25.9 us
    all_gather x1, blocking collectives, on_device(): lax.all_gather(jnp.concatenate([local_rows.reshape(1, -1), sums_part.resh...  5.18 us
    pallas_call x1, Pallas kernels, prepare(): pl.pallas_call(prep_kernel, grid_spec=pltpu.PrefetchScalarGridSpec(num_sc...  3.72 us
  transfers between devices with their start and end apart: 24, of which 11 were waited for; matrix products, arithmetic and copies ran while one was open for 6% of the time, Pallas kernels for 20%

profile of v3, /device:TPU:0, one launch (start us, length us, event | category | flops | bytes accessed | tf_op | source)
XLA Modules:
  0.0 157.5 jit_solution(5696773963278070804)
XLA Ops:
  0.6 1.3 broadcast_in_dim.133.tgt_ref
  1.9 3.7 %prep.1 = (bf16[96,2048]{1,0:T(8,128)(2,1)}, bf16[160,2048]{1,0:T(8,128)(2,1)}, bf16[160,2048]{1,0:T(8,128)(2,1)}) custom-call(s32[1]{0:T(128)} %bitcast.1.which, bf16[1536,2048]{1,0:T(8,128)(2,1)} %h3.1, bf16[1536,2048]{1,0:T(8,128)(2,1)} %h3.1, bf16[1536,2048]{1,0:T(8,128)(2,1)} %h3.1, bf16[1536,2048]{1,0:T(8,128)(2,1)} %h3.1, f32[1,2048]{1,0:T(1,128)} %bitcast.139, ...), custom_call_target="tpu_custom_call" | custom-call | flops 400000000 | bytes 3000000 | tf_op jit(solution)/shard_map/prep/pallas_call | solution.py:200
  5.7 1.5 fusion.34
  7.2 2.9 %collective-permute-start.4 = (bf16[256,2048]{1,0:T(8,128)(2,1)}, bf16[256,2048]{1,0:T(8,128)(2,1)}, u32[]{:S(2)}, u32[]{:S(2)}) collective-permute-start(bf16[256,2048]{1,0:T(8,128)(2,1)} %get-tuple-element.28), channel_id=1, source_target_pairs={{0,2},{1,3},{2,0},{3,1},{4,6},{5,7},{6,4},{7,5},{8,10},{9,11},{10,... | collective-permute-start | bytes 3145736 | tf_op jit(solution)/shard_map/ppermute | solution.py:119
  10.2 1.5 collective-permute-start.5
  11.7 2.6 %collective-permute-start = (bf16[160,2048]{1,0:T(8,128)(2,1)S(1)}, bf16[160,2048]{1,0:T(8,128)(2,1)S(1)}, u32[]{:S(2)}, u32[]{:S(2)}) collective-permute-start(bf16[160,2048]{1,0:T(8,128)(2,1)S(1)} %copy-done.11), channel_id=1, source_target_pairs={{0,16},{1,17},{2,18},{3,19},{4,20},{5,21},{6,22},{7,23},{8,24},{9,... | collective-permute-start | bytes 1966088 | tf_op jit(solution)/shard_map/ppermute | solution.py:119
  14.3 1.6 %collective-permute-start.1 = (bf16[96,2048]{1,0:T(8,128)(2,1)S(1)}, bf16[96,2048]{1,0:T(8,128)(2,1)S(1)}, u32[]{:S(2)}, u32[]{:S(2)}) collective-permute-start(bf16[96,2048]{1,0:T(8,128)(2,1)S(1)} %copy-done.12), channel_id=1, source_target_pairs={{0,8},{1,9},{2,10},{3,11},{4,12},{5,13},{6,14},{7,15},{8,0},{9,1},... | collective-permute-start | bytes 1179656 | tf_op jit(solution)/shard_map/ppermute | solution.py:119
  16.6 17.1 %collective-permute-done.4.refs_6_.refs_9_.refs_5_ = bf16[256,2048]{1,0:T(8,128)(2,1)} collective-permute-done((bf16[256,2048]{1,0:T(8,128)(2,1)}, bf16[256,2048]{1,0:T(8,128)(2,1)}, u32[]{:S(2)}, u32[]{:S(2)}) %collective-permute-start.4) | collective-permute-done | bytes 1048608 | tf_op jit(solution)/shard_map/ppermute | solution.py:119
  33.6 1.5 collective-permute-done.5.refs_8_.refs_11_.refs_7_
  35.4 1.7 %collective-permute-start.10 = (bf16[256,2048]{1,0:T(8,128)(2,1)}, bf16[256,2048]{1,0:T(8,128)(2,1)}, u32[]{:S(2)}, u32[]{:S(2)}) collective-permute-start(bf16[256,2048]{1,0:T(8,128)(2,1)} %get-tuple-element.28), channel_id=1, source_target_pairs={{0,4},{1,5},{2,6},{3,7},{4,0},{5,1},{6,2},{7,3},{8,12},{9,13},{10,... | collective-permute-start | bytes 3145736 | tf_op jit(solution)/shard_map/ppermute | solution.py:119
  37.2 1.4 clamp_reduce_fusion.1
  38.6 4.0 %collective-permute-done.traded_ref = bf16[160,2048]{1,0:T(8,128)(2,1)S(1)} collective-permute-done((bf16[160,2048]{1,0:T(8,128)(2,1)S(1)}, bf16[160,2048]{1,0:T(8,128)(2,1)S(1)}, u32[]{:S(2)}, u32[]{:S(2)}) %collective-permute-start) | collective-permute-done | bytes 655392 | tf_op jit(solution)/shard_map/ppermute | solution.py:119
  42.6 0.8 select_convert_fusion.sizes_ref
  43.4 3.0 %merge.1.refs_1_.refs_2_ = bf16[160,2048]{1,0:T(8,128)(2,1)} custom-call(s32[1]{0:T(128)} %bitcast.21.live_ref, bf16[160,2048]{1,0:T(8,128)(2,1)} %get-tuple-element.22.own_ref, bf16[160,2048]{1,0:T(8,128)(2,1)} %copy-done.4, f32[16,256]{1,0:T(8,128)} %select_convert_fusion.sizes_ref), custom_call_target="tpu_custom_call" | custom-call | flops 1000000 | bytes 3000000 | tf_op jit(solution)/shard_map/merge/pallas_call | solution.py:241
  46.4 3.9 %collective-permute-start.2 = (bf16[160,2048]{1,0:T(8,128)(2,1)}, bf16[160,2048]{1,0:T(8,128)(2,1)S(1)}, u32[]{:S(2)}, u32[]{:S(2)}) collective-permute-start(bf16[160,2048]{1,0:T(8,128)(2,1)} %merge.1.refs_1_.refs_2_), channel_id=1, source_target_pairs={{0,8},{1,9},{2,10},{3,11},{4,12},{5,13},{6,14},{7,15},{8,0},{9,1},... | collective-permute-start | bytes 1966088 | tf_op jit(solution)/shard_map/ppermute | solution.py:119
  50.3 11.8 %collective-permute-done.12.refs_5_ = bf16[96,2048]{1,0:T(8,128)(2,1)} collective-permute-done((bf16[96,2048]{1,0:T(8,128)(2,1)S(1)}, bf16[96,2048]{1,0:T(8,128)(2,1)}, u32[]{:S(2)}, u32[]{:S(2)}) %collective-permute-start.12) | collective-permute-done | bytes 393248 | tf_op jit(solution)/shard_map/ppermute | solution.py:119
  62.0 9.4 %collective-permute-done.2.refs_3_.refs_4_ = bf16[160,2048]{1,0:T(8,128)(2,1)S(1)} collective-permute-done((bf16[160,2048]{1,0:T(8,128)(2,1)}, bf16[160,2048]{1,0:T(8,128)(2,1)S(1)}, u32[]{:S(2)}, u32[]{:S(2)}) %collective-permute-start.2) | collective-permute-done | bytes 655392 | tf_op jit(solution)/shard_map/ppermute | solution.py:119
  73.0 1.5 collective-permute-done.7.refs_9_.refs_12_.refs_8_
  74.5 1.8 %collective-permute-start.13 = (bf16[160,2048]{1,0:T(8,128)(2,1)}, bf16[160,2048]{1,0:T(8,128)(2,1)}, u32[]{:S(2)}, u32[]{:S(2)}) collective-permute-start(bf16[160,2048]{1,0:T(8,128)(2,1)} %merge.1.refs_1_.refs_2_), channel_id=1, source_target_pairs={{0,16},{1,17},{2,18},{3,19},{4,20},{5,21},{6,22},{7,23},{8,24},{9,... | collective-permute-start | bytes 1966088 | tf_op jit(solution)/shard_map/ppermute | solution.py:119
  76.9 2.4 %collective-permute-start.14 = (bf16[96,2048]{1,0:T(8,128)(2,1)}, bf16[96,2048]{1,0:T(8,128)(2,1)S(1)}, u32[]{:S(2)}, u32[]{:S(2)}) collective-permute-start(bf16[96,2048]{1,0:T(8,128)(2,1)} %collective-permute-done.12.refs_5_), channel_id=1, source_target_pairs={{0,8},{1,9},{2,10},{3,11},{4,12},{5,13},{6,14},{7,15},{8,0},{9,1},... | collective-permute-start | bytes 1179656 | tf_op jit(solution)/shard_map/ppermute | solution.py:119
  79.3 13.8 %first.1.refs_0_ = f32[2,8,256]{2,1,0:T(8,128)} custom-call(s32[42]{0:T(128)} %concatenate.24.scalars, bf16[96,2048]{1,0:T(8,128)(2,1)} %get-tuple-element.29.refs_0_.refs_1_, bf16[160,2048]{1,0:T(8,128)(2,1)} %merge.1.refs_1_.refs_2_, bf16[96,2048]{1,0:T(8,128)(2,1)} %copy-done.13, bf16[160,2048]{1,0:T(8,128)(2,1)} %copy-done.10, ...), custom_call_target="tpu_custom_call" | custom-call | flops 6442450944 | bytes 14680064 | tf_op jit(solution)/shard_map/first/pallas_call | solution.py:412
  93.1 13.4 %collective-permute-done.13.refs_6_ = bf16[160,2048]{1,0:T(8,128)(2,1)} collective-permute-done((bf16[160,2048]{1,0:T(8,128)(2,1)}, bf16[160,2048]{1,0:T(8,128)(2,1)}, u32[]{:S(2)}, u32[]{:S(2)}) %collective-permute-start.13) | collective-permute-done | bytes 655392 | tf_op jit(solution)/shard_map/ppermute | solution.py:119
  109.4 1.5 collective-permute-done.18.refs_20_.refs_16_
  110.9 15.0 %second.1.refs_0_ = f32[3,8,256]{2,1,0:T(8,128)} custom-call(s32[46]{0:T(128)} %concatenate.23.scalars, f32[2,8,256]{2,1,0:T(8,128)} %first.1.refs_0_, bf16[96,2048]{1,0:T(8,128)(2,1)} %get-tuple-element.29.refs_0_.refs_1_, bf16[160,2048]{1,0:T(8,128)(2,1)} %merge.1.refs_1_.refs_2_, bf16[96,2048]{1,0:T(8,128)(2,1)} %copy-done.13, ...), custom_call_target="tpu_custom_call" | custom-call | flops 6442450944 | bytes 19922944 | tf_op jit(solution)/shard_map/second/pallas_call | solution.py:412
  126.0 0.8 copy-done.3
  126.8 11.2 %third.1 = f32[4,8,256]{2,1,0:T(8,128)} custom-call(s32[38]{0:T(128)} %concatenate.22.scalars, f32[3,8,256]{2,1,0:T(8,128)} %second.1.refs_0_, bf16[96,2048]{1,0:T(8,128)(2,1)} %copy-done.5, bf16[160,2048]{1,0:T(8,128)(2,1)} %copy-done.3, bf16[512,2048]{1,0:T(8,128)(2,1)} %refs_3_.1, bf16[512,2048]{1,0:T(8,128)(2,1)} %collective-permute-done.3.refs_5_.refs_8_.refs_4_, ...), custom_call_target="tpu_custom_call" | custom-call | flops 4294967296 | bytes 17825792 | tf_op jit(solution)/shard_map/third/pallas_call | solution.py:412
  138.0 2.7 %collective-permute-start.22 = (f32[4,8,256]{2,1,0:T(8,128)}, f32[4,8,256]{2,1,0:T(8,128)S(1)}, u32[]{:S(2)}, u32[]{:S(2)}) collective-permute-start(f32[4,8,256]{2,1,0:T(8,128)} %third.1), channel_id=1, source_target_pairs={{0,24},{1,25},{2,26},{3,27},{4,28},{5,29},{6,30},{7,31},{8,16},{9,... | collective-permute-start | bytes 98312 | tf_op jit(solution)/shard_map/ppermute | solution.py:119
  140.8 0.8 copy.52
  141.6 1.7 %collective-permute-start.20 = (f32[4,8,256]{2,0,1:T(4,128)S(1)}, f32[4,8,256]{2,0,1:T(4,128)S(1)}, u32[]{:S(2)}, u32[]{:S(2)}) collective-permute-start(f32[4,8,256]{2,0,1:T(4,128)S(1)} %copy.52), channel_id=1, source_target_pairs={{0,8},{1,9},{2,10},{3,11},{4,12},{5,13},{6,14},{7,15},{8,0},{9,1},... | collective-permute-start | bytes 98312 | tf_op jit(solution)/shard_map/ppermute | solution.py:119
  144.7 1.7 %collective-permute-done.21 = f32[4,8,256]{2,0,1:T(4,128)S(1)} collective-permute-done((f32[4,8,256]{2,0,1:T(4,128)S(1)}, f32[4,8,256]{2,0,1:T(4,128)S(1)}, u32[]{:S(2)}, u32[]{:S(2)}) %collective-permute-start.21) | collective-permute-done | bytes 32800 | tf_op jit(solution)/shard_map/ppermute | solution.py:119
  147.3 5.2 %all-gather.1 = f32[4,1,800]{2,1,0:T(1,128)S(1)} all-gather(f32[1,1,800]{2,1,0:T(1,128)S(1)} %maximum_bitcast_fusion), channel_id=2, replica_groups=mesh['tok'=8,'vocab'=4] {'vocab'}, dimensions={0}, use_global_device_ids=true | all-gather | bytes 16000 | tf_op jit(solution)/shard_map/all_gather | solution.py:561
  154.7 1.7 %collective-permute-done.23 = f32[4,24]{1,0:T(4,128)S(1)} collective-permute-done((f32[4,24]{1,0:T(4,128)S(1)}, f32[4,24]{1,0:T(4,128)S(1)}, u32[]{:S(2)}, u32[]{:S(2)}) %collective-permute-start.23) | collective-permute-done | bytes 416 | tf_op jit(solution)/shard_map/ppermute | solution.py:119
  (118 shorter events, 11.7 us)
Async XLA Ops:
  5.7 8.6 %copy-start.12 = (bf16[96,2048]{1,0:T(8,128)(2,1)S(1)}, bf16[96,2048]{1,0:T(8,128)(2,1)}, u32[]{:S(2)}) copy-start(bf16[96,2048]{1,0:T(8,128)(2,1)} %get-tuple-element.29.refs_0_.refs_1_) | copy-start | bytes 1179652
  5.7 10.2 %copy-start.14 = (s32[8,1]{0,1:T(1,128)S(1)}, s32[8,1]{0,1:T(1,128)}, u32[]{:S(2)}) copy-start(s32[8,1]{0,1:T(1,128)} %param.18) | copy-start | bytes 100
  5.7 10.2 %copy-start.15 = (s32[8]{0:T(128)S(1)}, s32[8]{0:T(128)}, u32[]{:S(2)}) copy-start(s32[8]{0:T(128)} %param.17) | copy-start | bytes 100
  7.2 69.0 %copy-start.7 = (s32[26]{0:T(128)S(1)}, s32[26]{0:T(128)}, u32[]{:S(2)}) copy-start(s32[26]{0:T(128)} %constant.120.clone) | copy-start | bytes 316
  7.2 26.4 %collective-permute-start.4 = (bf16[256,2048]{1,0:T(8,128)(2,1)}, bf16[256,2048]{1,0:T(8,128)(2,1)}, u32[]{:S(2)}, u32[]{:S(2)}) collective-permute-start(bf16[256,2048]{1,0:T(8,128)(2,1)} %get-tuple-element.28), channel_id=1, source_target_pairs={{0,2},{1,3},{2,0},{3,1},{4,6},{5,7},{6,4},{7,5},{8,10},{9,11},{10,... | collective-permute-start | bytes 3145736 | tf_op jit(solution)/shard_map/ppermute | solution.py:119
  10.2 24.9 %collective-permute-start.5 = (bf16[256,2048]{1,0:T(8,128)(2,1)}, bf16[256,2048]{1,0:T(8,128)(2,1)}, u32[]{:S(2)}, u32[]{:S(2)}) collective-permute-start(bf16[256,2048]{1,0:T(8,128)(2,1)} %get-tuple-element.27), channel_id=1, source_target_pairs={{0,4},{1,5},{2,6},{3,7},{4,0},{5,1},{6,2},{7,3},{8,12},{9,13},{10,... | collective-permute-start | bytes 3145736 | tf_op jit(solution)/shard_map/ppermute | solution.py:119
  11.7 30.9 %collective-permute-start = (bf16[160,2048]{1,0:T(8,128)(2,1)S(1)}, bf16[160,2048]{1,0:T(8,128)(2,1)S(1)}, u32[]{:S(2)}, u32[]{:S(2)}) collective-permute-start(bf16[160,2048]{1,0:T(8,128)(2,1)S(1)} %copy-done.11), channel_id=1, source_target_pairs={{0,16},{1,17},{2,18},{3,19},{4,20},{5,21},{6,22},{7,23},{8,24},{9,... | collective-permute-start | bytes 1966088 | tf_op jit(solution)/shard_map/ppermute | solution.py:119
  14.3 57.8 %collective-permute-start.3 = (bf16[512,2048]{1,0:T(8,128)(2,1)S(1)}, bf16[512,2048]{1,0:T(8,128)(2,1)}, u32[]{:S(2)}, u32[]{:S(2)}) collective-permute-start(bf16[512,2048]{1,0:T(8,128)(2,1)S(1)} %copy-done), channel_id=1, source_target_pairs={{0,1},{1,0},{2,3},{3,2},{4,5},{5,4},{6,7},{7,6},{8,9},{9,8},{10,11... | collective-permute-start | bytes 6291464 | tf_op jit(solution)/shard_map/ppermute | solution.py:119
  14.3 32.1 %collective-permute-start.1 = (bf16[96,2048]{1,0:T(8,128)(2,1)S(1)}, bf16[96,2048]{1,0:T(8,128)(2,1)S(1)}, u32[]{:S(2)}, u32[]{:S(2)}) collective-permute-start(bf16[96,2048]{1,0:T(8,128)(2,1)S(1)} %copy-done.12), channel_id=1, source_target_pairs={{0,8},{1,9},{2,10},{3,11},{4,12},{5,13},{6,14},{7,15},{8,0},{9,1},... | collective-permute-start | bytes 1179656 | tf_op jit(solution)/shard_map/ppermute | solution.py:119
  35.1 36.4 %collective-permute-start.8 = (bf16[256,2048]{1,0:T(8,128)(2,1)}, bf16[256,2048]{1,0:T(8,128)(2,1)}, u32[]{:S(2)}, u32[]{:S(2)}) collective-permute-start(bf16[256,2048]{1,0:T(8,128)(2,1)} %get-tuple-element.27), channel_id=1, source_target_pairs={{0,2},{1,3},{2,0},{3,1},{4,6},{5,7},{6,4},{7,5},{8,10},{9,11},{10,... | collective-permute-start | bytes 3145736 | tf_op jit(solution)/shard_map/ppermute | solution.py:119
  35.4 36.6 %collective-permute-start.10 = (bf16[256,2048]{1,0:T(8,128)(2,1)}, bf16[256,2048]{1,0:T(8,128)(2,1)}, u32[]{:S(2)}, u32[]{:S(2)}) collective-permute-start(bf16[256,2048]{1,0:T(8,128)(2,1)} %get-tuple-element.28), channel_id=1, source_target_pairs={{0,4},{1,5},{2,6},{3,7},{4,0},{5,1},{6,2},{7,3},{8,12},{9,13},{10,... | collective-permute-start | bytes 3145736 | tf_op jit(solution)/shard_map/ppermute | solution.py:119
  42.6 19.5 %collective-permute-start.12 = (bf16[96,2048]{1,0:T(8,128)(2,1)S(1)}, bf16[96,2048]{1,0:T(8,128)(2,1)}, u32[]{:S(2)}, u32[]{:S(2)}) collective-permute-start(bf16[96,2048]{1,0:T(8,128)(2,1)S(1)} %copy-done.12), channel_id=1, source_target_pairs={{0,16},{1,17},{2,18},{3,19},{4,20},{5,21},{6,22},{7,23},{8,24},{9,... | collective-permute-start | bytes 1179656 | tf_op jit(solution)/shard_map/ppermute | solution.py:119
  46.4 29.9 %copy-start.13 = (bf16[96,2048]{1,0:T(8,128)(2,1)}, bf16[96,2048]{1,0:T(8,128)(2,1)S(1)}, u32[]{:S(2)}) copy-start(bf16[96,2048]{1,0:T(8,128)(2,1)S(1)} %collective-permute-done.1.refs_2_.refs_3_) | copy-start | bytes 1179652
  46.4 25.1 %collective-permute-start.2 = (bf16[160,2048]{1,0:T(8,128)(2,1)}, bf16[160,2048]{1,0:T(8,128)(2,1)S(1)}, u32[]{:S(2)}, u32[]{:S(2)}) collective-permute-start(bf16[160,2048]{1,0:T(8,128)(2,1)} %merge.1.refs_1_.refs_2_), channel_id=1, source_target_pairs={{0,8},{1,9},{2,10},{3,11},{4,12},{5,13},{6,14},{7,15},{8,0},{9,1},... | collective-permute-start | bytes 1966088 | tf_op jit(solution)/shard_map/ppermute | solution.py:119
  62.0 10.6 %collective-permute-start.6 = (bf16[256,2048]{1,0:T(8,128)(2,1)}, bf16[256,2048]{1,0:T(8,128)(2,1)}, u32[]{:S(2)}, u32[]{:S(2)}) collective-permute-start(bf16[256,2048]{1,0:T(8,128)(2,1)} %collective-permute-done.4.refs_6_.refs_9_.refs_5_), channel_id=1, source_target_pairs={{0,1},{1,0},{2,3},{3,2},{4,5},{5,4},{6,7},{7,6},{8,9},{9,8},{10,11... | collective-permute-start | bytes 3145736 | tf_op jit(solution)/shard_map/ppermute | solution.py:119
  71.5 3.0 %collective-permute-start.7 = (bf16[256,2048]{1,0:T(8,128)(2,1)}, bf16[256,2048]{1,0:T(8,128)(2,1)}, u32[]{:S(2)}, u32[]{:S(2)}) collective-permute-start(bf16[256,2048]{1,0:T(8,128)(2,1)} %collective-permute-done.5.refs_8_.refs_11_.refs_7_), channel_id=1, source_target_pairs={{0,1},{1,0},{2,3},{3,2},{4,5},{5,4},{6,7},{7,6},{8,9},{9,8},{10,11... | collective-permute-start | bytes 3145736 | tf_op jit(solution)/shard_map/ppermute | solution.py:119
  71.5 5.4 %collective-permute-start.9 = (bf16[256,2048]{1,0:T(8,128)(2,1)}, bf16[256,2048]{1,0:T(8,128)(2,1)}, u32[]{:S(2)}, u32[]{:S(2)}) collective-permute-start(bf16[256,2048]{1,0:T(8,128)(2,1)} %collective-permute-done.8.refs_10_.refs_13_.refs_9_), channel_id=1, source_target_pairs={{0,1},{1,0},{2,3},{3,2},{4,5},{5,4},{6,7},{7,6},{8,9},{9,8},{10,11... | collective-permute-start | bytes 3145736 | tf_op jit(solution)/shard_map/ppermute | solution.py:119
  72.0 7.3 %collective-permute-start.11 = (bf16[256,2048]{1,0:T(8,128)(2,1)}, bf16[256,2048]{1,0:T(8,128)(2,1)}, u32[]{:S(2)}, u32[]{:S(2)}) collective-permute-start(bf16[256,2048]{1,0:T(8,128)(2,1)} %collective-permute-done.10.refs_12_.refs_15_.refs_11_), channel_id=1, source_target_pairs={{0,1},{1,0},{2,3},{3,2},{4,5},{5,4},{6,7},{7,6},{8,9},{9,8},{10,11... | collective-permute-start | bytes 3145736 | tf_op jit(solution)/shard_map/ppermute | solution.py:119
  72.1 34.5 %collective-permute-start.15 = (bf16[256,2048]{1,0:T(8,128)(2,1)}, bf16[256,2048]{1,0:T(8,128)(2,1)S(1)}, u32[]{:S(2)}, u32[]{:S(2)}) collective-permute-start(bf16[256,2048]{1,0:T(8,128)(2,1)} %collective-permute-done.5.refs_8_.refs_11_.refs_7_), channel_id=1, source_target_pairs={{0,2},{1,3},{2,0},{3,1},{4,6},{5,7},{6,4},{7,5},{8,10},{9,11},{10,... | collective-permute-start | bytes 3145736 | tf_op jit(solution)/shard_map/ppermute | solution.py:119
  72.7 33.9 %collective-permute-start.16 = (bf16[256,2048]{1,0:T(8,128)(2,1)}, bf16[256,2048]{1,0:T(8,128)(2,1)S(1)}, u32[]{:S(2)}, u32[]{:S(2)}) collective-permute-start(bf16[256,2048]{1,0:T(8,128)(2,1)} %collective-permute-done.4.refs_6_.refs_9_.refs_5_), channel_id=1, source_target_pairs={{0,4},{1,5},{2,6},{3,7},{4,0},{5,1},{6,2},{7,3},{8,12},{9,13},{10,... | collective-permute-start | bytes 3145736 | tf_op jit(solution)/shard_map/ppermute | solution.py:119
  74.5 32.0 %collective-permute-start.13 = (bf16[160,2048]{1,0:T(8,128)(2,1)}, bf16[160,2048]{1,0:T(8,128)(2,1)}, u32[]{:S(2)}, u32[]{:S(2)}) collective-permute-start(bf16[160,2048]{1,0:T(8,128)(2,1)} %merge.1.refs_1_.refs_2_), channel_id=1, source_target_pairs={{0,16},{1,17},{2,18},{3,19},{4,20},{5,21},{6,22},{7,23},{8,24},{9,... | collective-permute-start | bytes 1966088 | tf_op jit(solution)/shard_map/ppermute | solution.py:119
  76.9 31.2 %copy-start.9 = (s32[18]{0:T(128)S(1)}, s32[18]{0:T(128)}, u32[]{:S(2)}) copy-start(s32[18]{0:T(128)} %constant.123.clone) | copy-start | bytes 220
  76.9 31.8 %copy-start.8 = (s32[26]{0:T(128)S(1)}, s32[26]{0:T(128)}, u32[]{:S(2)}) copy-start(s32[26]{0:T(128)} %constant.122.clone) | copy-start | bytes 316
  76.9 29.6 %collective-permute-start.14 = (bf16[96,2048]{1,0:T(8,128)(2,1)}, bf16[96,2048]{1,0:T(8,128)(2,1)S(1)}, u32[]{:S(2)}, u32[]{:S(2)}) collective-permute-start(bf16[96,2048]{1,0:T(8,128)(2,1)} %collective-permute-done.12.refs_5_), channel_id=1, source_target_pairs={{0,8},{1,9},{2,10},{3,11},{4,12},{5,13},{6,14},{7,15},{8,0},{9,1},... | collective-permute-start | bytes 1179656 | tf_op jit(solution)/shard_map/ppermute | solution.py:119
  106.6 2.9 %collective-permute-start.17 = (bf16[256,2048]{1,0:T(8,128)(2,1)S(1)}, bf16[256,2048]{1,0:T(8,128)(2,1)}, u32[]{:S(2)}, u32[]{:S(2)}) collective-permute-start(bf16[256,2048]{1,0:T(8,128)(2,1)S(1)} %collective-permute-done.15.refs_17_.refs_13_), channel_id=1, source_target_pairs={{0,1},{1,0},{2,3},{3,2},{4,5},{5,4},{6,7},{7,6},{8,9},{9,8},{10,11... | collective-permute-start | bytes 3145736 | tf_op jit(solution)/shard_map/ppermute | solution.py:119
  106.7 4.3 %collective-permute-start.18 = (bf16[256,2048]{1,0:T(8,128)(2,1)S(1)}, bf16[256,2048]{1,0:T(8,128)(2,1)}, u32[]{:S(2)}, u32[]{:S(2)}) collective-permute-start(bf16[256,2048]{1,0:T(8,128)(2,1)S(1)} %collective-permute-done.16.refs_19_.refs_15_), channel_id=1, source_target_pairs={{0,1},{1,0},{2,3},{3,2},{4,5},{5,4},{6,7},{7,6},{8,9},{9,8},{10,11... | collective-permute-start | bytes 3145736 | tf_op jit(solution)/shard_map/ppermute | solution.py:119
  107.3 18.7 %collective-permute-start.19 = (bf16[160,2048]{1,0:T(8,128)(2,1)}, bf16[160,2048]{1,0:T(8,128)(2,1)S(1)}, u32[]{:S(2)}, u32[]{:S(2)}) collective-permute-start(bf16[160,2048]{1,0:T(8,128)(2,1)} %collective-permute-done.13.refs_6_), channel_id=1, source_target_pairs={{0,8},{1,9},{2,10},{3,11},{4,12},{5,13},{6,14},{7,15},{8,0},{9,1},... | collective-permute-start | bytes 1966088 | tf_op jit(solution)/shard_map/ppermute | solution.py:119
  126.0 18.6 %copy-start.6 = (s32[4]{0:T(128)S(1)}, s32[4]{0:T(128)}, u32[]{:S(2)}) copy-start(s32[4]{0:T(128)} %constant.124.clone) | copy-start | bytes 52
  138.0 6.7 %collective-permute-start.22 = (f32[4,8,256]{2,1,0:T(8,128)}, f32[4,8,256]{2,1,0:T(8,128)S(1)}, u32[]{:S(2)}, u32[]{:S(2)}) collective-permute-start(f32[4,8,256]{2,1,0:T(8,128)} %third.1), channel_id=1, source_target_pairs={{0,24},{1,25},{2,26},{3,27},{4,28},{5,29},{6,30},{7,31},{8,16},{9,... | collective-permute-start | bytes 98312 | tf_op jit(solution)/shard_map/ppermute | solution.py:119
  141.6 4.9 %collective-permute-start.21 = (f32[4,8,256]{2,0,1:T(4,128)S(1)}, f32[4,8,256]{2,0,1:T(4,128)S(1)}, u32[]{:S(2)}, u32[]{:S(2)}) collective-permute-start(f32[4,8,256]{2,0,1:T(4,128)S(1)} %copy.52), channel_id=1, source_target_pairs={{0,16},{1,17},{2,18},{3,19},{4,20},{5,21},{6,22},{7,23},{8,24},{9,... | collective-permute-start | bytes 98312 | tf_op jit(solution)/shard_map/ppermute | solution.py:119
  141.6 4.8 %collective-permute-start.20 = (f32[4,8,256]{2,0,1:T(4,128)S(1)}, f32[4,8,256]{2,0,1:T(4,128)S(1)}, u32[]{:S(2)}, u32[]{:S(2)}) collective-permute-start(f32[4,8,256]{2,0,1:T(4,128)S(1)} %copy.52), channel_id=1, source_target_pairs={{0,8},{1,9},{2,10},{3,11},{4,12},{5,13},{6,14},{7,15},{8,0},{9,1},... | collective-permute-start | bytes 98312 | tf_op jit(solution)/shard_map/ppermute | solution.py:119
  152.8 3.6 %collective-permute-start.23 = (f32[4,24]{1,0:T(4,128)S(1)}, f32[4,24]{1,0:T(4,128)S(1)}, u32[]{:S(2)}, u32[]{:S(2)}) collective-permute-start(f32[4,24]{1,0:T(4,128)S(1)} %pad_maximum_fusion), channel_id=1, source_target_pairs={{0,4},{1,5},{2,6},{3,7},{4,0},{5,1},{6,2},{7,3},{8,12},{9,13},{10,... | collective-permute-start | bytes 1160 | tf_op jit(solution)/shard_map/ppermute | solution.py:119
  (8 other events, 22.2 us)

commit v4 on v3

--- a/solution.py
+++ b/solution.py
@@ -147,7 +147,7 @@
 
 def prep_kernel(which, h0, h1, h2, h3, gain_ref, tgt_ref, sure_ref, own_ref, trade_ref):
     gain = gain_ref[...]
-    slots_count = tgt_ref.shape[1]
+    tgt_rows, tgt_lanes = tgt_ref.shape
     row = lax.broadcasted_iota(jnp.int32, (SURE, SURE), 0)
     col = lax.broadcasted_iota(jnp.int32, (SURE, SURE), 1)
     mirror = (row + col == SURE - 1).astype(jnp.bfloat16)
@@ -162,11 +162,8 @@
     trade_ref[0:SURE, :] = flip(normalize(h3[...], gain))
     trade_ref[SURE:REST, :] = flip(third)[0 : REST - SURE, :]
 
-    wanted = tgt_ref[...]
-    level = lax.broadcasted_iota(jnp.int32, (NOTES, slots_count), 0)
-    digits = jnp.where(level == 0, wanted & 127, jnp.where(level == 1, wanted >> 7, 0))
-    digits = digits.astype(jnp.float32).astype(jnp.bfloat16)
-    source = lax.broadcasted_iota(jnp.int32, (slots_count, TILE), 0)
+    level = lax.broadcasted_iota(jnp.int32, (NOTES, tgt_lanes), 0)
+    source = lax.broadcasted_iota(jnp.int32, (tgt_lanes, TILE), 0)
     lane = lax.broadcasted_iota(jnp.int32, (1, TILE), 1)
 
     def notes(local, keep):
@@ -177,8 +174,17 @@
         )
         at = local + block * ((VOCAB - 1) * SURE) + which[0] * SURE
         at = jnp.where(keep, at, -1)
-        pick = jnp.where(source == at, 1.0, 0.0).astype(jnp.bfloat16)
-        return jnp.dot(digits, pick, preferred_element_type=jnp.float32).astype(jnp.bfloat16)
+        found = jnp.zeros((NOTES, TILE), jnp.float32)
+        for row in range(tgt_rows):
+            wanted = tgt_ref[row : row + 1, :]
+            digits = jnp.where(level == 0, wanted & 127, jnp.where(level == 1, wanted >> 7, 0))
+            pick = jnp.where(source == at - row * tgt_lanes, 1.0, 0.0).astype(jnp.bfloat16)
+            found += jnp.dot(
+                digits.astype(jnp.float32).astype(jnp.bfloat16),
+                pick,
+                preferred_element_type=jnp.float32,
+            )
+        return found.astype(jnp.bfloat16)
 
     own_ref[REST : REST + NOTES, :] = jnp.zeros((NOTES, own_ref.shape[1]), jnp.bfloat16)
     own_ref[REST : REST + NOTES, 0:TILE] = notes(lane, lane < EVEN)
@@ -202,7 +208,7 @@
         grid_spec=pltpu.PrefetchScalarGridSpec(
             num_scalar_prefetch=1,
             grid=(1,),
-            in_specs=[block(j) for j in range(4)] + [whole(1, width), whole(1, targets.shape[0])],
+            in_specs=[block(j) for j in range(4)] + [whole(1, width), whole(*targets.shape)],
             out_specs=[whole(n, width) for n in (SURE, REST + NOTES, REST + NOTES)],
         ),
         out_shape=[
@@ -210,7 +216,7 @@
         ],
         cost_estimate=pl.CostEstimate(flops=4 * 10**8, bytes_accessed=3 * 10**6, transcendentals=SHARE),
         name="prep",
-    )(quarter.reshape(1), hidden, hidden, hidden, hidden, gain[None, :], targets[None, :])
+    )(quarter.reshape(1), hidden, hidden, hidden, hidden, gain[None, :], targets)
 
 
 def merge_kernel(live_ref, own_ref, traded_ref, sizes_ref, out_ref):
@@ -464,7 +470,7 @@
 
     zs = jnp.arange(NZ)
 
-    sure, rest_own, trade = prepare(hidden, gain, targets, quarter)
+    sure, rest_own, trade = prepare(hidden, gain, targets.reshape(-1, 128), quarter)
     traded = across(trade, 2)
     sizes_own = after(jnp.concatenate([lengths, group_map[:, 0]]), sure)
     load = jnp.sum(sizes_own[:8])

time: 158 us -> 157 us (level)
  no operation moved by 1% of the time
where the time goes in v4:
time: 157 us; the launch traced here: 156 us
  waiting for transfers between devices  63.7 us (41%)
  Pallas kernels  46.8 us (30%)
  starting transfers between devices  25.8 us (16%)
  local copies, waits for them, and re-layouts  8.1 us (5%)
  other arithmetic  5.75 us (4%)
  blocking collectives  5.18 us (3%)
    ppermute x24, waiting for transfers between devices, send(): return lax.ppermute(value, BOTH, device_pairs(target))  63.7 us
    pallas_call x3, Pallas kernels, statistics(): pl.pallas_call(functools.partial(stats_kernel, units, len(sets), n_known,...  40.1 us
    ppermute x24, starting transfers between devices, send(): return lax.ppermute(value, BOTH, device_pairs(target))  25.8 us
    all_gather x1, blocking collectives, on_device(): lax.all_gather(jnp.concatenate([local_rows.reshape(1, -1), sums_part.resh...  5.18 us
    pallas_call x1, Pallas kernels, prepare(): pl.pallas_call(prep_kernel, grid_spec=pltpu.PrefetchScalarGridSpec(num_sc...  3.77 us
  transfers between devices with their start and end apart: 24, of which 11 were waited for; matrix products, arithmetic and copies ran while one was open for 6% of the time, Pallas kernels for 20%

profile of v4, /device:TPU:0, one launch (start us, length us, event | category | flops | bytes accessed | tf_op | source)
XLA Modules:
  0.0 156.3 jit_solution(10736171450497436394)
XLA Ops:
  0.7 3.8 %prep.1 = (bf16[96,2048]{1,0:T(8,128)(2,1)}, bf16[160,2048]{1,0:T(8,128)(2,1)}, bf16[160,2048]{1,0:T(8,128)(2,1)}) custom-call(s32[1]{0:T(128)} %bitcast.1.which, bf16[1536,2048]{1,0:T(8,128)(2,1)} %h3.1, bf16[1536,2048]{1,0:T(8,128)(2,1)} %h3.1, bf16[1536,2048]{1,0:T(8,128)(2,1)} %h3.1, bf16[1536,2048]{1,0:T(8,128)(2,1)} %h3.1, f32[1,2048]{1,0:T(1,128)} %bitcast.140, ...), custom_call_target="tpu_custom_call" | custom-call | flops 400000000 | bytes 3000000 | tf_op jit(solution)/shard_map/prep/pallas_call | solution.py:206
  4.5 1.5 fusion.34
  6.0 2.9 %collective-permute-start.4 = (bf16[256,2048]{1,0:T(8,128)(2,1)}, bf16[256,2048]{1,0:T(8,128)(2,1)}, u32[]{:S(2)}, u32[]{:S(2)}) collective-permute-start(bf16[256,2048]{1,0:T(8,128)(2,1)} %get-tuple-element.28), channel_id=1, source_target_pairs={{0,2},{1,3},{2,0},{3,1},{4,6},{5,7},{6,4},{7,5},{8,10},{9,11},{10,... | collective-permute-start | bytes 3145736 | tf_op jit(solution)/shard_map/ppermute | solution.py:119
  9.0 1.5 collective-permute-start.5
  10.5 2.6 %collective-permute-start = (bf16[160,2048]{1,0:T(8,128)(2,1)S(1)}, bf16[160,2048]{1,0:T(8,128)(2,1)S(1)}, u32[]{:S(2)}, u32[]{:S(2)}) collective-permute-start(bf16[160,2048]{1,0:T(8,128)(2,1)S(1)} %copy-done.11), channel_id=1, source_target_pairs={{0,16},{1,17},{2,18},{3,19},{4,20},{5,21},{6,22},{7,23},{8,24},{9,... | collective-permute-start | bytes 1966088 | tf_op jit(solution)/shard_map/ppermute | solution.py:119
  13.1 1.6 %collective-permute-start.1 = (bf16[96,2048]{1,0:T(8,128)(2,1)S(1)}, bf16[96,2048]{1,0:T(8,128)(2,1)S(1)}, u32[]{:S(2)}, u32[]{:S(2)}) collective-permute-start(bf16[96,2048]{1,0:T(8,128)(2,1)S(1)} %copy-done.12), channel_id=1, source_target_pairs={{0,8},{1,9},{2,10},{3,11},{4,12},{5,13},{6,14},{7,15},{8,0},{9,1},... | collective-permute-start | bytes 1179656 | tf_op jit(solution)/shard_map/ppermute | solution.py:119
  15.4 17.1 %collective-permute-done.4.refs_6_.refs_9_.refs_5_ = bf16[256,2048]{1,0:T(8,128)(2,1)} collective-permute-done((bf16[256,2048]{1,0:T(8,128)(2,1)}, bf16[256,2048]{1,0:T(8,128)(2,1)}, u32[]{:S(2)}, u32[]{:S(2)}) %collective-permute-start.4) | collective-permute-done | bytes 1048608 | tf_op jit(solution)/shard_map/ppermute | solution.py:119
  32.4 1.5 collective-permute-done.5.refs_8_.refs_11_.refs_7_
  34.2 1.7 %collective-permute-start.10 = (bf16[256,2048]{1,0:T(8,128)(2,1)}, bf16[256,2048]{1,0:T(8,128)(2,1)}, u32[]{:S(2)}, u32[]{:S(2)}) collective-permute-start(bf16[256,2048]{1,0:T(8,128)(2,1)} %get-tuple-element.28), channel_id=1, source_target_pairs={{0,4},{1,5},{2,6},{3,7},{4,0},{5,1},{6,2},{7,3},{8,12},{9,13},{10,... | collective-permute-start | bytes 3145736 | tf_op jit(solution)/shard_map/ppermute | solution.py:119
  35.9 1.4 clamp_reduce_fusion.1
  37.3 4.0 %collective-permute-done.traded_ref = bf16[160,2048]{1,0:T(8,128)(2,1)S(1)} collective-permute-done((bf16[160,2048]{1,0:T(8,128)(2,1)S(1)}, bf16[160,2048]{1,0:T(8,128)(2,1)S(1)}, u32[]{:S(2)}, u32[]{:S(2)}) %collective-permute-start) | collective-permute-done | bytes 655392 | tf_op jit(solution)/shard_map/ppermute | solution.py:119
  41.3 0.8 select_convert_fusion.sizes_ref
  42.2 3.0 %merge.1.refs_1_.refs_2_ = bf16[160,2048]{1,0:T(8,128)(2,1)} custom-call(s32[1]{0:T(128)} %bitcast.22.live_ref, bf16[160,2048]{1,0:T(8,128)(2,1)} %get-tuple-element.22.own_ref, bf16[160,2048]{1,0:T(8,128)(2,1)} %copy-done.4, f32[16,256]{1,0:T(8,128)} %select_convert_fusion.sizes_ref), custom_call_target="tpu_custom_call" | custom-call | flops 1000000 | bytes 3000000 | tf_op jit(solution)/shard_map/merge/pallas_call | solution.py:247
  45.1 3.9 %collective-permute-start.2 = (bf16[160,2048]{1,0:T(8,128)(2,1)}, bf16[160,2048]{1,0:T(8,128)(2,1)S(1)}, u32[]{:S(2)}, u32[]{:S(2)}) collective-permute-start(bf16[160,2048]{1,0:T(8,128)(2,1)} %merge.1.refs_1_.refs_2_), channel_id=1, source_target_pairs={{0,8},{1,9},{2,10},{3,11},{4,12},{5,13},{6,14},{7,15},{8,0},{9,1},... | collective-permute-start | bytes 1966088 | tf_op jit(solution)/shard_map/ppermute | solution.py:119
  49.0 11.8 %collective-permute-done.12.refs_5_ = bf16[96,2048]{1,0:T(8,128)(2,1)} collective-permute-done((bf16[96,2048]{1,0:T(8,128)(2,1)S(1)}, bf16[96,2048]{1,0:T(8,128)(2,1)}, u32[]{:S(2)}, u32[]{:S(2)}) %collective-permute-start.12) | collective-permute-done | bytes 393248 | tf_op jit(solution)/shard_map/ppermute | solution.py:119
  60.8 9.4 %collective-permute-done.2.refs_3_.refs_4_ = bf16[160,2048]{1,0:T(8,128)(2,1)S(1)} collective-permute-done((bf16[160,2048]{1,0:T(8,128)(2,1)}, bf16[160,2048]{1,0:T(8,128)(2,1)S(1)}, u32[]{:S(2)}, u32[]{:S(2)}) %collective-permute-start.2) | collective-permute-done | bytes 655392 | tf_op jit(solution)/shard_map/ppermute | solution.py:119
  71.8 1.5 collective-permute-done.7.refs_9_.refs_12_.refs_8_
  73.3 1.7 %collective-permute-start.13 = (bf16[160,2048]{1,0:T(8,128)(2,1)}, bf16[160,2048]{1,0:T(8,128)(2,1)}, u32[]{:S(2)}, u32[]{:S(2)}) collective-permute-start(bf16[160,2048]{1,0:T(8,128)(2,1)} %merge.1.refs_1_.refs_2_), channel_id=1, source_target_pairs={{0,16},{1,17},{2,18},{3,19},{4,20},{5,21},{6,22},{7,23},{8,24},{9,... | collective-permute-start | bytes 1966088 | tf_op jit(solution)/shard_map/ppermute | solution.py:119
  75.6 2.4 %collective-permute-start.14 = (bf16[96,2048]{1,0:T(8,128)(2,1)}, bf16[96,2048]{1,0:T(8,128)(2,1)S(1)}, u32[]{:S(2)}, u32[]{:S(2)}) collective-permute-start(bf16[96,2048]{1,0:T(8,128)(2,1)} %collective-permute-done.12.refs_5_), channel_id=1, source_target_pairs={{0,8},{1,9},{2,10},{3,11},{4,12},{5,13},{6,14},{7,15},{8,0},{9,1},... | collective-permute-start | bytes 1179656 | tf_op jit(solution)/shard_map/ppermute | solution.py:119
  78.0 13.8 %first.1.refs_0_ = f32[2,8,256]{2,1,0:T(8,128)} custom-call(s32[42]{0:T(128)} %concatenate.24.scalars, bf16[96,2048]{1,0:T(8,128)(2,1)} %get-tuple-element.29.refs_0_.refs_1_, bf16[160,2048]{1,0:T(8,128)(2,1)} %merge.1.refs_1_.refs_2_, bf16[96,2048]{1,0:T(8,128)(2,1)} %copy-done.13, bf16[160,2048]{1,0:T(8,128)(2,1)} %copy-done.10, ...), custom_call_target="tpu_custom_call" | custom-call | flops 6442450944 | bytes 14680064 | tf_op jit(solution)/shard_map/first/pallas_call | solution.py:418
  91.9 13.5 %collective-permute-done.13.refs_6_ = bf16[160,2048]{1,0:T(8,128)(2,1)} collective-permute-done((bf16[160,2048]{1,0:T(8,128)(2,1)}, bf16[160,2048]{1,0:T(8,128)(2,1)}, u32[]{:S(2)}, u32[]{:S(2)}) %collective-permute-start.13) | collective-permute-done | bytes 655392 | tf_op jit(solution)/shard_map/ppermute | solution.py:119
  108.2 1.5 collective-permute-done.18.refs_20_.refs_16_
  109.7 15.0 %second.1.refs_0_ = f32[3,8,256]{2,1,0:T(8,128)} custom-call(s32[46]{0:T(128)} %concatenate.23.scalars, f32[2,8,256]{2,1,0:T(8,128)} %first.1.refs_0_, bf16[96,2048]{1,0:T(8,128)(2,1)} %get-tuple-element.29.refs_0_.refs_1_, bf16[160,2048]{1,0:T(8,128)(2,1)} %merge.1.refs_1_.refs_2_, bf16[96,2048]{1,0:T(8,128)(2,1)} %copy-done.13, ...), custom_call_target="tpu_custom_call" | custom-call | flops 6442450944 | bytes 19922944 | tf_op jit(solution)/shard_map/second/pallas_call | solution.py:418
  124.8 0.8 copy-done.3
  125.7 11.2 %third.1 = f32[4,8,256]{2,1,0:T(8,128)} custom-call(s32[38]{0:T(128)} %concatenate.22.scalars, f32[3,8,256]{2,1,0:T(8,128)} %second.1.refs_0_, bf16[96,2048]{1,0:T(8,128)(2,1)} %copy-done.5, bf16[160,2048]{1,0:T(8,128)(2,1)} %copy-done.3, bf16[512,2048]{1,0:T(8,128)(2,1)} %refs_3_.1, bf16[512,2048]{1,0:T(8,128)(2,1)} %collective-permute-done.3.refs_5_.refs_8_.refs_4_, ...), custom_call_target="tpu_custom_call" | custom-call | flops 4294967296 | bytes 17825792 | tf_op jit(solution)/shard_map/third/pallas_call | solution.py:418
  136.8 2.7 %collective-permute-start.22 = (f32[4,8,256]{2,1,0:T(8,128)}, f32[4,8,256]{2,1,0:T(8,128)S(1)}, u32[]{:S(2)}, u32[]{:S(2)}) collective-permute-start(f32[4,8,256]{2,1,0:T(8,128)} %third.1), channel_id=1, source_target_pairs={{0,24},{1,25},{2,26},{3,27},{4,28},{5,29},{6,30},{7,31},{8,16},{9,... | collective-permute-start | bytes 98312 | tf_op jit(solution)/shard_map/ppermute | solution.py:119
  139.5 0.8 copy.52
  140.4 1.8 %collective-permute-start.20 = (f32[4,8,256]{2,0,1:T(4,128)S(1)}, f32[4,8,256]{2,0,1:T(4,128)S(1)}, u32[]{:S(2)}, u32[]{:S(2)}) collective-permute-start(f32[4,8,256]{2,0,1:T(4,128)S(1)} %copy.52), channel_id=1, source_target_pairs={{0,8},{1,9},{2,10},{3,11},{4,12},{5,13},{6,14},{7,15},{8,0},{9,1},... | collective-permute-start | bytes 98312 | tf_op jit(solution)/shard_map/ppermute | solution.py:119
  142.2 0.7 slice_convert_fusion.1
  143.5 1.7 %collective-permute-done.21 = f32[4,8,256]{2,0,1:T(4,128)S(1)} collective-permute-done((f32[4,8,256]{2,0,1:T(4,128)S(1)}, f32[4,8,256]{2,0,1:T(4,128)S(1)}, u32[]{:S(2)}, u32[]{:S(2)}) %collective-permute-start.21) | collective-permute-done | bytes 32800 | tf_op jit(solution)/shard_map/ppermute | solution.py:119
  146.1 5.2 %all-gather.1 = f32[4,1,800]{2,1,0:T(1,128)S(1)} all-gather(f32[1,1,800]{2,1,0:T(1,128)S(1)} %maximum_bitcast_fusion), channel_id=2, replica_groups=mesh['tok'=8,'vocab'=4] {'vocab'}, dimensions={0}, use_global_device_ids=true | all-gather | bytes 16000 | tf_op jit(solution)/shard_map/all_gather | solution.py:567
  153.5 1.7 %collective-permute-done.23 = f32[4,24]{1,0:T(4,128)S(1)} collective-permute-done((f32[4,24]{1,0:T(4,128)S(1)}, f32[4,24]{1,0:T(4,128)S(1)}, u32[]{:S(2)}, u32[]{:S(2)}) %collective-permute-start.23) | collective-permute-done | bytes 416 | tf_op jit(solution)/shard_map/ppermute | solution.py:119
  (117 shorter events, 10.9 us)
Async XLA Ops:
  4.5 8.6 %copy-start.12 = (bf16[96,2048]{1,0:T(8,128)(2,1)S(1)}, bf16[96,2048]{1,0:T(8,128)(2,1)}, u32[]{:S(2)}) copy-start(bf16[96,2048]{1,0:T(8,128)(2,1)} %get-tuple-element.29.refs_0_.refs_1_) | copy-start | bytes 1179652
  4.5 10.2 %copy-start.14 = (s32[8,1]{0,1:T(1,128)S(1)}, s32[8,1]{0,1:T(1,128)}, u32[]{:S(2)}) copy-start(s32[8,1]{0,1:T(1,128)} %param.18) | copy-start | bytes 100
  4.5 10.2 %copy-start.15 = (s32[8]{0:T(128)S(1)}, s32[8]{0:T(128)}, u32[]{:S(2)}) copy-start(s32[8]{0:T(128)} %param.17) | copy-start | bytes 100
  6.0 69.0 %copy-start.7 = (s32[26]{0:T(128)S(1)}, s32[26]{0:T(128)}, u32[]{:S(2)}) copy-start(s32[26]{0:T(128)} %constant.120.clone) | copy-start | bytes 316
  6.0 26.4 %collective-permute-start.4 = (bf16[256,2048]{1,0:T(8,128)(2,1)}, bf16[256,2048]{1,0:T(8,128)(2,1)}, u32[]{:S(2)}, u32[]{:S(2)}) collective-permute-start(bf16[256,2048]{1,0:T(8,128)(2,1)} %get-tuple-element.28), channel_id=1, source_target_pairs={{0,2},{1,3},{2,0},{3,1},{4,6},{5,7},{6,4},{7,5},{8,10},{9,11},{10,... | collective-permute-start | bytes 3145736 | tf_op jit(solution)/shard_map/ppermute | solution.py:119
  9.0 24.9 %collective-permute-start.5 = (bf16[256,2048]{1,0:T(8,128)(2,1)}, bf16[256,2048]{1,0:T(8,128)(2,1)}, u32[]{:S(2)}, u32[]{:S(2)}) collective-permute-start(bf16[256,2048]{1,0:T(8,128)(2,1)} %get-tuple-element.27), channel_id=1, source_target_pairs={{0,4},{1,5},{2,6},{3,7},{4,0},{5,1},{6,2},{7,3},{8,12},{9,13},{10,... | collective-permute-start | bytes 3145736 | tf_op jit(solution)/shard_map/ppermute | solution.py:119
  10.5 30.9 %collective-permute-start = (bf16[160,2048]{1,0:T(8,128)(2,1)S(1)}, bf16[160,2048]{1,0:T(8,128)(2,1)S(1)}, u32[]{:S(2)}, u32[]{:S(2)}) collective-permute-start(bf16[160,2048]{1,0:T(8,128)(2,1)S(1)} %copy-done.11), channel_id=1, source_target_pairs={{0,16},{1,17},{2,18},{3,19},{4,20},{5,21},{6,22},{7,23},{8,24},{9,... | collective-permute-start | bytes 1966088 | tf_op jit(solution)/shard_map/ppermute | solution.py:119
  13.1 57.8 %collective-permute-start.3 = (bf16[512,2048]{1,0:T(8,128)(2,1)S(1)}, bf16[512,2048]{1,0:T(8,128)(2,1)}, u32[]{:S(2)}, u32[]{:S(2)}) collective-permute-start(bf16[512,2048]{1,0:T(8,128)(2,1)S(1)} %copy-done), channel_id=1, source_target_pairs={{0,1},{1,0},{2,3},{3,2},{4,5},{5,4},{6,7},{7,6},{8,9},{9,8},{10,11... | collective-permute-start | bytes 6291464 | tf_op jit(solution)/shard_map/ppermute | solution.py:119
  13.1 32.1 %collective-permute-start.1 = (bf16[96,2048]{1,0:T(8,128)(2,1)S(1)}, bf16[96,2048]{1,0:T(8,128)(2,1)S(1)}, u32[]{:S(2)}, u32[]{:S(2)}) collective-permute-start(bf16[96,2048]{1,0:T(8,128)(2,1)S(1)} %copy-done.12), channel_id=1, source_target_pairs={{0,8},{1,9},{2,10},{3,11},{4,12},{5,13},{6,14},{7,15},{8,0},{9,1},... | collective-permute-start | bytes 1179656 | tf_op jit(solution)/shard_map/ppermute | solution.py:119
  33.9 36.4 %collective-permute-start.8 = (bf16[256,2048]{1,0:T(8,128)(2,1)}, bf16[256,2048]{1,0:T(8,128)(2,1)}, u32[]{:S(2)}, u32[]{:S(2)}) collective-permute-start(bf16[256,2048]{1,0:T(8,128)(2,1)} %get-tuple-element.27), channel_id=1, source_target_pairs={{0,2},{1,3},{2,0},{3,1},{4,6},{5,7},{6,4},{7,5},{8,10},{9,11},{10,... | collective-permute-start | bytes 3145736 | tf_op jit(solution)/shard_map/ppermute | solution.py:119
  34.2 36.6 %collective-permute-start.10 = (bf16[256,2048]{1,0:T(8,128)(2,1)}, bf16[256,2048]{1,0:T(8,128)(2,1)}, u32[]{:S(2)}, u32[]{:S(2)}) collective-permute-start(bf16[256,2048]{1,0:T(8,128)(2,1)} %get-tuple-element.28), channel_id=1, source_target_pairs={{0,4},{1,5},{2,6},{3,7},{4,0},{5,1},{6,2},{7,3},{8,12},{9,13},{10,... | collective-permute-start | bytes 3145736 | tf_op jit(solution)/shard_map/ppermute | solution.py:119
  41.3 19.5 %collective-permute-start.12 = (bf16[96,2048]{1,0:T(8,128)(2,1)S(1)}, bf16[96,2048]{1,0:T(8,128)(2,1)}, u32[]{:S(2)}, u32[]{:S(2)}) collective-permute-start(bf16[96,2048]{1,0:T(8,128)(2,1)S(1)} %copy-done.12), channel_id=1, source_target_pairs={{0,16},{1,17},{2,18},{3,19},{4,20},{5,21},{6,22},{7,23},{8,24},{9,... | collective-permute-start | bytes 1179656 | tf_op jit(solution)/shard_map/ppermute | solution.py:119
  45.1 29.9 %copy-start.13 = (bf16[96,2048]{1,0:T(8,128)(2,1)}, bf16[96,2048]{1,0:T(8,128)(2,1)S(1)}, u32[]{:S(2)}) copy-start(bf16[96,2048]{1,0:T(8,128)(2,1)S(1)} %collective-permute-done.1.refs_2_.refs_3_) | copy-start | bytes 1179652
  45.1 25.1 %collective-permute-start.2 = (bf16[160,2048]{1,0:T(8,128)(2,1)}, bf16[160,2048]{1,0:T(8,128)(2,1)S(1)}, u32[]{:S(2)}, u32[]{:S(2)}) collective-permute-start(bf16[160,2048]{1,0:T(8,128)(2,1)} %merge.1.refs_1_.refs_2_), channel_id=1, source_target_pairs={{0,8},{1,9},{2,10},{3,11},{4,12},{5,13},{6,14},{7,15},{8,0},{9,1},... | collective-permute-start | bytes 1966088 | tf_op jit(solution)/shard_map/ppermute | solution.py:119
  60.8 10.6 %collective-permute-start.6 = (bf16[256,2048]{1,0:T(8,128)(2,1)}, bf16[256,2048]{1,0:T(8,128)(2,1)}, u32[]{:S(2)}, u32[]{:S(2)}) collective-permute-start(bf16[256,2048]{1,0:T(8,128)(2,1)} %collective-permute-done.4.refs_6_.refs_9_.refs_5_), channel_id=1, source_target_pairs={{0,1},{1,0},{2,3},{3,2},{4,5},{5,4},{6,7},{7,6},{8,9},{9,8},{10,11... | collective-permute-start | bytes 3145736 | tf_op jit(solution)/shard_map/ppermute | solution.py:119
  70.3 3.0 %collective-permute-start.7 = (bf16[256,2048]{1,0:T(8,128)(2,1)}, bf16[256,2048]{1,0:T(8,128)(2,1)}, u32[]{:S(2)}, u32[]{:S(2)}) collective-permute-start(bf16[256,2048]{1,0:T(8,128)(2,1)} %collective-permute-done.5.refs_8_.refs_11_.refs_7_), channel_id=1, source_target_pairs={{0,1},{1,0},{2,3},{3,2},{4,5},{5,4},{6,7},{7,6},{8,9},{9,8},{10,11... | collective-permute-start | bytes 3145736 | tf_op jit(solution)/shard_map/ppermute | solution.py:119
  70.3 5.3 %collective-permute-start.9 = (bf16[256,2048]{1,0:T(8,128)(2,1)}, bf16[256,2048]{1,0:T(8,128)(2,1)}, u32[]{:S(2)}, u32[]{:S(2)}) collective-permute-start(bf16[256,2048]{1,0:T(8,128)(2,1)} %collective-permute-done.8.refs_10_.refs_13_.refs_9_), channel_id=1, source_target_pairs={{0,1},{1,0},{2,3},{3,2},{4,5},{5,4},{6,7},{7,6},{8,9},{9,8},{10,11... | collective-permute-start | bytes 3145736 | tf_op jit(solution)/shard_map/ppermute | solution.py:119
  70.8 7.2 %collective-permute-start.11 = (bf16[256,2048]{1,0:T(8,128)(2,1)}, bf16[256,2048]{1,0:T(8,128)(2,1)}, u32[]{:S(2)}, u32[]{:S(2)}) collective-permute-start(bf16[256,2048]{1,0:T(8,128)(2,1)} %collective-permute-done.10.refs_12_.refs_15_.refs_11_), channel_id=1, source_target_pairs={{0,1},{1,0},{2,3},{3,2},{4,5},{5,4},{6,7},{7,6},{8,9},{9,8},{10,11... | collective-permute-start | bytes 3145736 | tf_op jit(solution)/shard_map/ppermute | solution.py:119
  70.9 34.5 %collective-permute-start.15 = (bf16[256,2048]{1,0:T(8,128)(2,1)}, bf16[256,2048]{1,0:T(8,128)(2,1)S(1)}, u32[]{:S(2)}, u32[]{:S(2)}) collective-permute-start(bf16[256,2048]{1,0:T(8,128)(2,1)} %collective-permute-done.5.refs_8_.refs_11_.refs_7_), channel_id=1, source_target_pairs={{0,2},{1,3},{2,0},{3,1},{4,6},{5,7},{6,4},{7,5},{8,10},{9,11},{10,... | collective-permute-start | bytes 3145736 | tf_op jit(solution)/shard_map/ppermute | solution.py:119
  71.4 34.0 %collective-permute-start.16 = (bf16[256,2048]{1,0:T(8,128)(2,1)}, bf16[256,2048]{1,0:T(8,128)(2,1)S(1)}, u32[]{:S(2)}, u32[]{:S(2)}) collective-permute-start(bf16[256,2048]{1,0:T(8,128)(2,1)} %collective-permute-done.4.refs_6_.refs_9_.refs_5_), channel_id=1, source_target_pairs={{0,4},{1,5},{2,6},{3,7},{4,0},{5,1},{6,2},{7,3},{8,12},{9,13},{10,... | collective-permute-start | bytes 3145736 | tf_op jit(solution)/shard_map/ppermute | solution.py:119
  73.3 32.0 %collective-permute-start.13 = (bf16[160,2048]{1,0:T(8,128)(2,1)}, bf16[160,2048]{1,0:T(8,128)(2,1)}, u32[]{:S(2)}, u32[]{:S(2)}) collective-permute-start(bf16[160,2048]{1,0:T(8,128)(2,1)} %merge.1.refs_1_.refs_2_), channel_id=1, source_target_pairs={{0,16},{1,17},{2,18},{3,19},{4,20},{5,21},{6,22},{7,23},{8,24},{9,... | collective-permute-start | bytes 1966088 | tf_op jit(solution)/shard_map/ppermute | solution.py:119
  75.6 31.2 %copy-start.9 = (s32[18]{0:T(128)S(1)}, s32[18]{0:T(128)}, u32[]{:S(2)}) copy-start(s32[18]{0:T(128)} %constant.123.clone) | copy-start | bytes 220
  75.6 31.9 %copy-start.8 = (s32[26]{0:T(128)S(1)}, s32[26]{0:T(128)}, u32[]{:S(2)}) copy-start(s32[26]{0:T(128)} %constant.122.clone) | copy-start | bytes 316
  75.6 29.7 %collective-permute-start.14 = (bf16[96,2048]{1,0:T(8,128)(2,1)}, bf16[96,2048]{1,0:T(8,128)(2,1)S(1)}, u32[]{:S(2)}, u32[]{:S(2)}) collective-permute-start(bf16[96,2048]{1,0:T(8,128)(2,1)} %collective-permute-done.12.refs_5_), channel_id=1, source_target_pairs={{0,8},{1,9},{2,10},{3,11},{4,12},{5,13},{6,14},{7,15},{8,0},{9,1},... | collective-permute-start | bytes 1179656 | tf_op jit(solution)/shard_map/ppermute | solution.py:119
  105.4 2.9 %collective-permute-start.17 = (bf16[256,2048]{1,0:T(8,128)(2,1)S(1)}, bf16[256,2048]{1,0:T(8,128)(2,1)}, u32[]{:S(2)}, u32[]{:S(2)}) collective-permute-start(bf16[256,2048]{1,0:T(8,128)(2,1)S(1)} %collective-permute-done.15.refs_17_.refs_13_), channel_id=1, source_target_pairs={{0,1},{1,0},{2,3},{3,2},{4,5},{5,4},{6,7},{7,6},{8,9},{9,8},{10,11... | collective-permute-start | bytes 3145736 | tf_op jit(solution)/shard_map/ppermute | solution.py:119
  105.5 4.3 %collective-permute-start.18 = (bf16[256,2048]{1,0:T(8,128)(2,1)S(1)}, bf16[256,2048]{1,0:T(8,128)(2,1)}, u32[]{:S(2)}, u32[]{:S(2)}) collective-permute-start(bf16[256,2048]{1,0:T(8,128)(2,1)S(1)} %collective-permute-done.16.refs_19_.refs_15_), channel_id=1, source_target_pairs={{0,1},{1,0},{2,3},{3,2},{4,5},{5,4},{6,7},{7,6},{8,9},{9,8},{10,11... | collective-permute-start | bytes 3145736 | tf_op jit(solution)/shard_map/ppermute | solution.py:119
  106.1 18.7 %collective-permute-start.19 = (bf16[160,2048]{1,0:T(8,128)(2,1)}, bf16[160,2048]{1,0:T(8,128)(2,1)S(1)}, u32[]{:S(2)}, u32[]{:S(2)}) collective-permute-start(bf16[160,2048]{1,0:T(8,128)(2,1)} %collective-permute-done.13.refs_6_), channel_id=1, source_target_pairs={{0,8},{1,9},{2,10},{3,11},{4,12},{5,13},{6,14},{7,15},{8,0},{9,1},... | collective-permute-start | bytes 1966088 | tf_op jit(solution)/shard_map/ppermute | solution.py:119
  124.8 18.6 %copy-start.6 = (s32[4]{0:T(128)S(1)}, s32[4]{0:T(128)}, u32[]{:S(2)}) copy-start(s32[4]{0:T(128)} %constant.124.clone) | copy-start | bytes 52
  136.8 6.7 %collective-permute-start.22 = (f32[4,8,256]{2,1,0:T(8,128)}, f32[4,8,256]{2,1,0:T(8,128)S(1)}, u32[]{:S(2)}, u32[]{:S(2)}) collective-permute-start(f32[4,8,256]{2,1,0:T(8,128)} %third.1), channel_id=1, source_target_pairs={{0,24},{1,25},{2,26},{3,27},{4,28},{5,29},{6,30},{7,31},{8,16},{9,... | collective-permute-start | bytes 98312 | tf_op jit(solution)/shard_map/ppermute | solution.py:119
  140.3 4.9 %collective-permute-start.21 = (f32[4,8,256]{2,0,1:T(4,128)S(1)}, f32[4,8,256]{2,0,1:T(4,128)S(1)}, u32[]{:S(2)}, u32[]{:S(2)}) collective-permute-start(f32[4,8,256]{2,0,1:T(4,128)S(1)} %copy.52), channel_id=1, source_target_pairs={{0,16},{1,17},{2,18},{3,19},{4,20},{5,21},{6,22},{7,23},{8,24},{9,... | collective-permute-start | bytes 98312 | tf_op jit(solution)/shard_map/ppermute | solution.py:119
  140.4 4.8 %collective-permute-start.20 = (f32[4,8,256]{2,0,1:T(4,128)S(1)}, f32[4,8,256]{2,0,1:T(4,128)S(1)}, u32[]{:S(2)}, u32[]{:S(2)}) collective-permute-start(f32[4,8,256]{2,0,1:T(4,128)S(1)} %copy.52), channel_id=1, source_target_pairs={{0,8},{1,9},{2,10},{3,11},{4,12},{5,13},{6,14},{7,15},{8,0},{9,1},... | collective-permute-start | bytes 98312 | tf_op jit(solution)/shard_map/ppermute | solution.py:119
  151.6 3.6 %collective-permute-start.23 = (f32[4,24]{1,0:T(4,128)S(1)}, f32[4,24]{1,0:T(4,128)S(1)}, u32[]{:S(2)}, u32[]{:S(2)}) collective-permute-start(f32[4,24]{1,0:T(4,128)S(1)} %pad_maximum_fusion), channel_id=1, source_target_pairs={{0,4},{1,5},{2,6},{3,7},{4,0},{5,1},{6,2},{7,3},{8,12},{9,13},{10,... | collective-permute-start | bytes 1160 | tf_op jit(solution)/shard_map/ppermute | solution.py:119
  (8 other events, 22.2 us)
